TPU v7x, 768 devices: a whole 4x8x12 slice. The times are simulated.
768 devices in a mesh: ctx: 192 (over y, z, core), head: 4 (over x).
Axes of the slice: x: 4, y: 8, z: 12, core: 2. Of those that a mesh axis runs over, the one named last changes fastest.
Arguments:
- queries: bfloat16 [49152, 256], P('ctx', 'head'), may hold values from -6 to 6
- keys: bfloat16 [49152, 256], P('ctx', 'head'), may hold values from -6 to 6
- values: bfloat16 [49152, 2048], P('ctx', 'head'), may hold values from -6 to 6
- conv_keys: float32 [3, 256], P(None, 'head'), may hold values from -3.5 to 3.5
- conv_values: float32 [3, 2048], P(None, 'head'), may hold values from -3.5 to 3.5
- out_weight: bfloat16 [2048, 2048], P('head'), may hold values from -0.125 to 0.125
- cotangent: bfloat16 [49152, 2048], P('ctx', 'head'), may hold values from -6 to 6
Outputs:
- mixed_out: bfloat16 [49152, 2048], P('ctx', 'head')
- value_grad: bfloat16 [49152, 2048], P('ctx', 'head')
All inputs are finite; a program needn't handle non-finite values.
Results may differ from a plain program's by a relative error of at most 0.004.
The roundings to bfloat16 on the way count: a program that leaves them out, or rounds other values in their place, can miss the bound.
Values may be sent and summed in bfloat16 or wider, within the bound.
A program may use at most 32 MiB of HBM per device.

v0:
```python
import jax
import jax.numpy as jnp
from jax import lax
from jax.sharding import PartitionSpec as P

FEAT = 16
VDIM = 128
CONV = 3


def shifted(x, axis, by):
    peers = lax.axis_size(axis)
    pairs = [(i, i + by) for i in range(peers) if 0 <= i + by < peers]
    return lax.ppermute(x, axis, pairs)


def features(rows_in, head_count):
    grid = rows_in.T.reshape(head_count, FEAT, rows_in.shape[0]) * FEAT ** (-0.25)
    square = grid[:, :, None, :] * grid[:, None, :, :]
    square = square.reshape(head_count, FEAT * FEAT, rows_in.shape[0]) * 0.5**0.5
    constant = jnp.ones((head_count, 1, rows_in.shape[0]), jnp.float32)
    return jnp.concatenate([constant, grid, square], 1).astype(jnp.bfloat16)


def convolve(token_block, before, weights):
    joined = jnp.concatenate([before, token_block], 0).astype(jnp.float32)
    block_rows = token_block.shape[0]
    running = weights[0] * joined[CONV - 1 : CONV - 1 + block_rows]
    for offset in range(1, CONV):
        running = (
            running + weights[offset] * joined[CONV - 1 - offset : CONV - 1 - offset + block_rows]
        )
    return running


def per_device(queries, keys, values, conv_keys, conv_values, out_weight, cotangent):
    highest = lax.Precision.HIGHEST
    block_rows = queries.shape[0]
    head_count = queries.shape[1] // FEAT
    key_width = keys.shape[1]
    slab_count = lax.axis_size("ctx")
    last_rows = jnp.concatenate(
        [keys[block_rows - (CONV - 1) :], values[block_rows - (CONV - 1) :]], 1
    )
    before = shifted(last_rows, "ctx", 1)
    key_conv = convolve(keys, before[:, :key_width], conv_keys)
    value_conv = convolve(values, before[:, key_width:], conv_values).astype(jnp.bfloat16)
    query_feat = features(queries.astype(jnp.float32), head_count)
    key_feat = features(key_conv, head_count)
    value_heads = value_conv.reshape(block_rows, head_count, VDIM)
    causal = jnp.arange(block_rows)[:, None] >= jnp.arange(block_rows)[None, :]
    scores = jnp.einsum("hpt,hps->hts", query_feat, key_feat, preferred_element_type=jnp.float32)
    scores = jnp.where(causal[None], scores, 0.0)
    weight_low = scores.astype(jnp.bfloat16)
    block_state = jnp.einsum(
        "hps,shv->hpv", key_feat, value_heads, preferred_element_type=jnp.float32
    )
    block_norm = jnp.sum(key_feat.astype(jnp.float32), 2)
    running = (block_state, block_norm)
    distance = 1
    while distance < slab_count:
        moved = shifted((running[0], running[1]), "ctx", distance)
        running = (running[0] + moved[0], running[1] + moved[1])
        distance = distance * 2
    prior_state = running[0] - block_state
    prior_norm = running[1] - block_norm
    numerator = jnp.einsum(
        "hts,shv->thv", weight_low, value_heads, preferred_element_type=jnp.float32
    )
    numerator = numerator + jnp.einsum(
        "hpt,hpv->thv",
        query_feat,
        prior_state.astype(jnp.bfloat16),
        preferred_element_type=jnp.float32,
    )
    denominator = jnp.sum(scores, 2).T + jnp.einsum(
        "hpt,hp->th", query_feat.astype(jnp.float32), prior_norm, precision=highest
    )
    attended = (
        (numerator / denominator[..., None])
        .astype(jnp.bfloat16)
        .reshape(block_rows, head_count * VDIM)
    )
    head_terms = jnp.dot(attended, out_weight, preferred_element_type=jnp.float32)
    mixed_out = lax.psum_scatter(head_terms, "head", scatter_dimension=1, tiled=True).astype(
        jnp.bfloat16
    )
    whole_grad = lax.all_gather(cotangent, "head", axis=1, tiled=True)
    out_grad = jnp.einsum("td,cd->tc", whole_grad, out_weight, preferred_element_type=jnp.float32)
    scaled_grad = (out_grad.reshape(block_rows, head_count, VDIM) / denominator[..., None]).astype(
        jnp.bfloat16
    )
    block_query = jnp.einsum(
        "hpt,thv->hpv", query_feat, scaled_grad, preferred_element_type=jnp.float32
    )
    total_later = block_query
    distance = 1
    while distance < slab_count:
        total_later = total_later + shifted(total_later, "ctx", -distance)
        distance = distance * 2
    later_state = total_later - block_query
    value_grad = jnp.einsum(
        "hts,thv->shv", weight_low, scaled_grad, preferred_element_type=jnp.float32
    )
    value_grad = value_grad + jnp.einsum(
        "hps,hpv->shv",
        key_feat,
        later_state.astype(jnp.bfloat16),
        preferred_element_type=jnp.float32,
    )
    return (mixed_out, value_grad.astype(jnp.bfloat16).reshape(block_rows, head_count * VDIM))


def solution(mesh):
    in_specs = (
        P("ctx", "head"),
        P("ctx", "head"),
        P("ctx", "head"),
        P(None, "head"),
        P(None, "head"),
        P("head", None),
        P("ctx", "head"),
    )
    out_specs = (P("ctx", "head"), P("ctx", "head"))
    return jax.shard_map(
        per_device, mesh=mesh, in_specs=in_specs, out_specs=out_specs, check_vma=False
    )
```

profile of v0, /device:TPU:22, one launch (start us, length us, event | category | flops | bytes accessed | tf_op | source)
XLA Modules:
  0.0 641.2 jit_solution(17655165702371992922)
XLA Ops:
  9.1 1.9 collective-permute-start
  12.6 11.6 %collective-permute-done = bf16[2,576]{1,0:T(2,128)(2,1)S(1)} collective-permute-done((bf16[2,576]{1,0:T(2,128)(2,1)S(1)}, bf16[2,576]{1,0:T(2,128)(2,1)S(1)}, u32[]{:S(2)}, u32[]{:S(2)}) %collective-permute-start) | collective-permute-done | bytes 2336 | tf_op jit(solution)/shard_map/ppermute | solution.py:14
  26.6 1.9 collective-permute-start.1
  28.5 11.1 %collective-permute-done.1 = f32[4,273,128]{2,0,1:T(4,128)S(1)} collective-permute-done((f32[4,273,128]{2,0,1:T(4,128)S(1)}, f32[4,273,128]{2,0,1:T(4,128)S(1)}, u32[]{:S(2)}, u32[]{:S(2)}) %collective-permute-start.1) | collective-permute-done | bytes 559136 | tf_op jit(solution)/shard_map/ppermute | solution.py:14
  39.8 1.9 collective-permute-start.2
  41.7 12.5 %collective-permute-done.2 = f32[4,273,128]{2,0,1:T(4,128)S(1)} collective-permute-done((f32[4,273,128]{2,0,1:T(4,128)S(1)}, f32[4,273,128]{2,0,1:T(4,128)S(1)}, u32[]{:S(2)}, u32[]{:S(2)}) %collective-permute-start.2) | collective-permute-done | bytes 559136 | tf_op jit(solution)/shard_map/ppermute | solution.py:14
  59.5 22.3 %collective-permute-done.9 = f32[4,273]{1,0:T(4,128)S(1)} collective-permute-done((f32[4,273]{1,0:T(4,128)S(1)}, f32[4,273]{1,0:T(4,128)S(1)}, u32[]{:S(2)}, u32[]{:S(2)}) %collective-permute-start.9) | collective-permute-done | bytes 4400 | tf_op jit(solution)/shard_map/ppermute | solution.py:14
  83.8 5.6 collective-permute-done.10
  91.4 6.6 %collective-permute-done.11 = f32[4,273]{1,0:T(4,128)S(1)} collective-permute-done((f32[4,273]{1,0:T(4,128)S(1)}, f32[4,273]{1,0:T(4,128)S(1)}, u32[]{:S(2)}, u32[]{:S(2)}) %collective-permute-start.11) | collective-permute-done | bytes 4400 | tf_op jit(solution)/shard_map/ppermute | solution.py:14
  100.0 8.3 %collective-permute-done.12 = f32[4,273]{1,0:T(4,128)S(1)} collective-permute-done((f32[4,273]{1,0:T(4,128)S(1)}, f32[4,273]{1,0:T(4,128)S(1)}, u32[]{:S(2)}, u32[]{:S(2)}) %collective-permute-start.12) | collective-permute-done | bytes 4400 | tf_op jit(solution)/shard_map/ppermute | solution.py:14
  108.3 2.5 collective-permute-start.13
  112.0 8.3 %collective-permute-start.4 = (f32[4,273,128]{2,0,1:T(4,128)S(1)}, f32[4,273,128]{2,0,1:T(4,128)S(1)}, u32[]{:S(2)}, u32[]{:S(2)}) collective-permute-start(f32[4,273,128]{2,0,1:T(4,128)S(1)} %copy.29), channel_id=1, source_target_pairs={{0,32},{4,36},{8,40},{12,44},{16,48},{20,52},{24,56},{28,60},{32,6... | collective-permute-start | bytes 1677320 | tf_op jit(solution)/shard_map/ppermute | solution.py:14
  120.4 10.1 %collective-permute-start.14 = (f32[4,273]{1,0:T(4,128)S(1)}, f32[4,273]{1,0:T(4,128)S(1)}, u32[]{:S(2)}, u32[]{:S(2)}) collective-permute-start(f32[4,273]{1,0:T(4,128)S(1)} %add.120), channel_id=1, source_target_pairs={{0,128},{4,132},{8,136},{12,140},{16,144},{20,148},{24,152},{28,15... | collective-permute-start | bytes 13112 | tf_op jit(solution)/shard_map/ppermute | solution.py:14
  130.5 30.8 %collective-permute-done.14 = f32[4,273]{1,0:T(4,128)S(1)} collective-permute-done((f32[4,273]{1,0:T(4,128)S(1)}, f32[4,273]{1,0:T(4,128)S(1)}, u32[]{:S(2)}, u32[]{:S(2)}) %collective-permute-start.14) | collective-permute-done | bytes 4400 | tf_op jit(solution)/shard_map/ppermute | solution.py:14
  161.3 9.3 %collective-permute-start.15 = (f32[4,273]{1,0:T(4,128)S(1)}, f32[4,273]{1,0:T(4,128)S(1)}, u32[]{:S(2)}, u32[]{:S(2)}) collective-permute-start(f32[4,273]{1,0:T(4,128)S(1)} %add.121), channel_id=1, source_target_pairs={{0,256},{4,260},{8,264},{12,268},{16,272},{20,276},{24,280},{28,28... | collective-permute-start | bytes 13112 | tf_op jit(solution)/shard_map/ppermute | solution.py:14
  172.3 9.4 %collective-permute-start.16 = (f32[4,273]{1,0:T(4,128)S(1)}, f32[4,273]{1,0:T(4,128)S(1)}, u32[]{:S(2)}, u32[]{:S(2)}) collective-permute-start(f32[4,273]{1,0:T(4,128)S(1)} %add.122), channel_id=1, source_target_pairs={{0,512},{4,516},{8,520},{12,524},{16,528},{20,532},{24,536},{28,54... | collective-permute-start | bytes 13112 | tf_op jit(solution)/shard_map/ppermute | solution.py:14
  184.4 48.2 %collective-permute-done.5 = f32[4,273,128]{2,0,1:T(4,128)S(1)} collective-permute-done((f32[4,273,128]{2,0,1:T(4,128)S(1)}, f32[4,273,128]{2,0,1:T(4,128)S(1)}, u32[]{:S(2)}, u32[]{:S(2)}) %collective-permute-start.5) | collective-permute-done | bytes 559136 | tf_op jit(solution)/shard_map/ppermute | solution.py:14
  235.5 2.0 fusion.33
  241.3 24.6 %collective-permute-done.6 = f32[4,273,128]{2,0,1:T(4,128)} collective-permute-done((f32[4,273,128]{2,0,1:T(4,128)}, f32[4,273,128]{2,0,1:T(4,128)}, u32[]{:S(2)}, u32[]{:S(2)}) %collective-permute-start.6) | collective-permute-done | bytes 559136 | tf_op jit(solution)/shard_map/ppermute | solution.py:14
  267.2 9.6 %collective-permute-start.7 = (f32[4,273,128]{2,0,1:T(4,128)S(1)}, f32[4,273,128]{2,0,1:T(4,128)S(1)}, u32[]{:S(2)}, u32[]{:S(2)}) collective-permute-start(f32[4,273,128]{2,0,1:T(4,128)S(1)} %copy.35), channel_id=1, source_target_pairs={{0,256},{4,260},{8,264},{12,268},{16,272},{20,276},{24,280},{28,28... | collective-permute-start | bytes 1677320 | tf_op jit(solution)/shard_map/ppermute | solution.py:14
  277.0 2.1 collective-permute-start.18
  279.1 39.7 %collective-permute-done.7 = f32[4,273,128]{2,0,1:T(4,128)S(1)} collective-permute-done((f32[4,273,128]{2,0,1:T(4,128)S(1)}, f32[4,273,128]{2,0,1:T(4,128)S(1)}, u32[]{:S(2)}, u32[]{:S(2)}) %collective-permute-start.7) | collective-permute-done | bytes 559136 | tf_op jit(solution)/shard_map/ppermute | solution.py:14
  320.6 12.0 %collective-permute-done.18 = f32[4,273,128]{2,0,1:T(4,128)S(1)} collective-permute-done((f32[4,273,128]{2,0,1:T(4,128)S(1)}, f32[4,273,128]{2,0,1:T(4,128)S(1)}, u32[]{:S(2)}, u32[]{:S(2)}) %collective-permute-start.18) | collective-permute-done | bytes 559136 | tf_op jit(solution)/shard_map/ppermute | solution.py:14
  336.2 2.1 fusion.32
  338.3 28.9 %collective-permute-done.19 = f32[4,273,128]{2,0,1:T(4,128)} collective-permute-done((f32[4,273,128]{2,0,1:T(4,128)}, f32[4,273,128]{2,0,1:T(4,128)}, u32[]{:S(2)}, u32[]{:S(2)}) %collective-permute-start.19) | collective-permute-done | bytes 559136 | tf_op jit(solution)/shard_map/ppermute | solution.py:14
  370.4 20.1 %collective-permute-done.20 = f32[4,273,128]{2,0,1:T(4,128)S(1)} collective-permute-done((f32[4,273,128]{2,0,1:T(4,128)S(1)}, f32[4,273,128]{2,0,1:T(4,128)S(1)}, u32[]{:S(2)}, u32[]{:S(2)}) %collective-permute-start.20) | collective-permute-done | bytes 559136 | tf_op jit(solution)/shard_map/ppermute | solution.py:14
  390.7 1.9 collective-permute-start.21
  392.6 68.1 %collective-permute-done.21 = f32[4,273,128]{2,0,1:T(4,128)S(1)} collective-permute-done((f32[4,273,128]{2,0,1:T(4,128)S(1)}, f32[4,273,128]{2,0,1:T(4,128)S(1)}, u32[]{:S(2)}, u32[]{:S(2)}) %collective-permute-start.21) | collective-permute-done | bytes 559136 | tf_op jit(solution)/shard_map/ppermute | solution.py:14
  460.9 1.9 collective-permute-start.22
  462.8 22.4 %collective-permute-done.22 = f32[4,273,128]{2,0,1:T(4,128)S(1)} collective-permute-done((f32[4,273,128]{2,0,1:T(4,128)S(1)}, f32[4,273,128]{2,0,1:T(4,128)S(1)}, u32[]{:S(2)}, u32[]{:S(2)}) %collective-permute-start.22) | collective-permute-done | bytes 559136 | tf_op jit(solution)/shard_map/ppermute | solution.py:14
  486.9 114.5 %collective-permute-done.23 = f32[4,273,128]{2,0,1:T(4,128)S(1)} collective-permute-done((f32[4,273,128]{2,0,1:T(4,128)S(1)}, f32[4,273,128]{2,0,1:T(4,128)S(1)}, u32[]{:S(2)}, u32[]{:S(2)}) %collective-permute-start.23) | collective-permute-done | bytes 559136 | tf_op jit(solution)/shard_map/ppermute | solution.py:14
  603.4 27.8 %collective-permute-done.24 = f32[4,273,128]{2,0,1:T(4,128)S(1)} collective-permute-done((f32[4,273,128]{2,0,1:T(4,128)S(1)}, f32[4,273,128]{2,0,1:T(4,128)S(1)}, u32[]{:S(2)}, u32[]{:S(2)}) %collective-permute-start.24) | collective-permute-done | bytes 559136 | tf_op jit(solution)/shard_map/ppermute | solution.py:14
  (126 shorter events, 46.6 us)
Async XLA Ops:
  7.2 228.4 %copy-start = (bf16[512,2048]{1,0:T(8,128)(2,1)S(1)}, bf16[512,2048]{1,0:T(8,128)(2,1)}, u32[]{:S(2)}) copy-start(bf16[512,2048]{1,0:T(8,128)(2,1)} %param.12) | copy-start | bytes 6291460
  7.2 228.3 %all-gather.2.cloned.1.call-start = ((), (), s32[]{:S(2)}) async-start(), calls=%async_computation.2 | async-start | bytes 1310720 | tf_op jit(solution)/shard_map/all_gather | solution.py:88
  9.1 15.2 %collective-permute-start = (bf16[2,576]{1,0:T(2,128)(2,1)S(1)}, bf16[2,576]{1,0:T(2,128)(2,1)S(1)}, u32[]{:S(2)}, u32[]{:S(2)}) collective-permute-start(bf16[2,576]{1,0:T(2,128)(2,1)S(1)} %pad_maximum_fusion.2), channel_id=1, source_target_pairs={{0,4},{4,8},{8,12},{12,16},{16,20},{20,24},{24,28},{28,32},{32,36}... | collective-permute-start | bytes 6920 | tf_op jit(solution)/shard_map/ppermute | solution.py:14
  25.6 145.1 %copy-start.1 = (bf16[4,16,16,256]{3,2,1,0:T(8,128)(2,1)}, bf16[4,16,16,256]{3,2,1,0:T(8,128)(2,1)S(1)}, u32[]{:S(2)}) copy-start(bf16[4,16,16,256]{3,2,1,0:T(8,128)(2,1)S(1)} %multiply_convert_fusion) | copy-start | bytes 1572868
  26.6 13.0 %collective-permute-start.1 = (f32[4,273,128]{2,0,1:T(4,128)S(1)}, f32[4,273,128]{2,0,1:T(4,128)S(1)}, u32[]{:S(2)}, u32[]{:S(2)}) collective-permute-start(f32[4,273,128]{2,0,1:T(4,128)S(1)} %copy.23), channel_id=1, source_target_pairs={{0,4},{4,8},{8,12},{12,16},{16,20},{20,24},{24,28},{28,32},{32,36}... | collective-permute-start | bytes 1677320 | tf_op jit(solution)/shard_map/ppermute | solution.py:14
  39.8 14.4 %collective-permute-start.2 = (f32[4,273,128]{2,0,1:T(4,128)S(1)}, f32[4,273,128]{2,0,1:T(4,128)S(1)}, u32[]{:S(2)}, u32[]{:S(2)}) collective-permute-start(f32[4,273,128]{2,0,1:T(4,128)S(1)} %copy.25), channel_id=1, source_target_pairs={{0,8},{4,12},{8,16},{12,20},{16,24},{20,28},{24,32},{28,36},{32,40... | collective-permute-start | bytes 1677320 | tf_op jit(solution)/shard_map/ppermute | solution.py:14
  55.2 55.6 %collective-permute-start.3 = (f32[4,273,128]{2,0,1:T(4,128)}, f32[4,273,128]{2,0,1:T(4,128)}, u32[]{:S(2)}, u32[]{:S(2)}) collective-permute-start(f32[4,273,128]{2,0,1:T(4,128)} %copy.27), channel_id=1, source_target_pairs={{0,16},{4,20},{8,24},{12,28},{16,32},{20,36},{24,40},{28,44},{32,4... | collective-permute-start | bytes 1677320 | tf_op jit(solution)/shard_map/ppermute | solution.py:14
  57.6 24.2 %collective-permute-start.9 = (f32[4,273]{1,0:T(4,128)S(1)}, f32[4,273]{1,0:T(4,128)S(1)}, u32[]{:S(2)}, u32[]{:S(2)}) collective-permute-start(f32[4,273]{1,0:T(4,128)S(1)} %convert_reduce_fusion), channel_id=1, source_target_pairs={{0,4},{4,8},{8,12},{12,16},{16,20},{20,24},{24,28},{28,32},{32,36}... | collective-permute-start | bytes 13112 | tf_op jit(solution)/shard_map/ppermute | solution.py:14
  81.8 7.6 %collective-permute-start.10 = (f32[4,273]{1,0:T(4,128)S(1)}, f32[4,273]{1,0:T(4,128)S(1)}, u32[]{:S(2)}, u32[]{:S(2)}) collective-permute-start(f32[4,273]{1,0:T(4,128)S(1)} %add.116), channel_id=1, source_target_pairs={{0,8},{4,12},{8,16},{12,20},{16,24},{20,28},{24,32},{28,36},{32,40... | collective-permute-start | bytes 13112 | tf_op jit(solution)/shard_map/ppermute | solution.py:14
  83.7 548.9 %reduce-scatter.2.cloned.1.call-start = ((), (), s32[]{:S(2)}) async-start(), calls=%async_computation.1 | async-start | bytes 2621440 | tf_op jit(solution)/shard_map/reduce_scatter | solution.py:85
  89.4 8.5 %collective-permute-start.11 = (f32[4,273]{1,0:T(4,128)S(1)}, f32[4,273]{1,0:T(4,128)S(1)}, u32[]{:S(2)}, u32[]{:S(2)}) collective-permute-start(f32[4,273]{1,0:T(4,128)S(1)} %add.117), channel_id=1, source_target_pairs={{0,16},{4,20},{8,24},{12,28},{16,32},{20,36},{24,40},{28,44},{32,4... | collective-permute-start | bytes 13112 | tf_op jit(solution)/shard_map/ppermute | solution.py:14
  98.0 10.3 %collective-permute-start.12 = (f32[4,273]{1,0:T(4,128)S(1)}, f32[4,273]{1,0:T(4,128)S(1)}, u32[]{:S(2)}, u32[]{:S(2)}) collective-permute-start(f32[4,273]{1,0:T(4,128)S(1)} %add.118), channel_id=1, source_target_pairs={{0,32},{4,36},{8,40},{12,44},{16,48},{20,52},{24,56},{28,60},{32,6... | collective-permute-start | bytes 13112 | tf_op jit(solution)/shard_map/ppermute | solution.py:14
  100.0 83.9 %copy-start.5 = (bf16[4,16,16,256]{3,2,1,0:T(8,128)(2,1)}, bf16[4,16,16,256]{3,2,1,0:T(8,128)(2,1)S(1)}, u32[]{:S(2)}) copy-start(bf16[4,16,16,256]{3,2,1,0:T(8,128)(2,1)S(1)} %multiply_convert_fusion.1) | copy-start | bytes 1572868
  108.3 12.1 %collective-permute-start.13 = (f32[4,273]{1,0:T(4,128)S(1)}, f32[4,273]{1,0:T(4,128)S(1)}, u32[]{:S(2)}, u32[]{:S(2)}) collective-permute-start(f32[4,273]{1,0:T(4,128)S(1)} %add.119), channel_id=1, source_target_pairs={{0,64},{4,68},{8,72},{12,76},{16,80},{20,84},{24,88},{28,92},{32,9... | collective-permute-start | bytes 13112 | tf_op jit(solution)/shard_map/ppermute | solution.py:14
  112.0 69.6 %collective-permute-start.4 = (f32[4,273,128]{2,0,1:T(4,128)S(1)}, f32[4,273,128]{2,0,1:T(4,128)S(1)}, u32[]{:S(2)}, u32[]{:S(2)}) collective-permute-start(f32[4,273,128]{2,0,1:T(4,128)S(1)} %copy.29), channel_id=1, source_target_pairs={{0,32},{4,36},{8,40},{12,44},{16,48},{20,52},{24,56},{28,60},{32,6... | collective-permute-start | bytes 1677320 | tf_op jit(solution)/shard_map/ppermute | solution.py:14
  120.4 41.0 %collective-permute-start.14 = (f32[4,273]{1,0:T(4,128)S(1)}, f32[4,273]{1,0:T(4,128)S(1)}, u32[]{:S(2)}, u32[]{:S(2)}) collective-permute-start(f32[4,273]{1,0:T(4,128)S(1)} %add.120), channel_id=1, source_target_pairs={{0,128},{4,132},{8,136},{12,140},{16,144},{20,148},{24,152},{28,15... | collective-permute-start | bytes 13112 | tf_op jit(solution)/shard_map/ppermute | solution.py:14
  161.3 10.9 %collective-permute-start.15 = (f32[4,273]{1,0:T(4,128)S(1)}, f32[4,273]{1,0:T(4,128)S(1)}, u32[]{:S(2)}, u32[]{:S(2)}) collective-permute-start(f32[4,273]{1,0:T(4,128)S(1)} %add.121), channel_id=1, source_target_pairs={{0,256},{4,260},{8,264},{12,268},{16,272},{20,276},{24,280},{28,28... | collective-permute-start | bytes 13112 | tf_op jit(solution)/shard_map/ppermute | solution.py:14
  172.3 11.6 %collective-permute-start.16 = (f32[4,273]{1,0:T(4,128)S(1)}, f32[4,273]{1,0:T(4,128)S(1)}, u32[]{:S(2)}, u32[]{:S(2)}) collective-permute-start(f32[4,273]{1,0:T(4,128)S(1)} %add.122), channel_id=1, source_target_pairs={{0,512},{4,516},{8,520},{12,524},{16,528},{20,532},{24,536},{28,54... | collective-permute-start | bytes 13112 | tf_op jit(solution)/shard_map/ppermute | solution.py:14
  181.9 50.7 %collective-permute-start.5 = (f32[4,273,128]{2,0,1:T(4,128)S(1)}, f32[4,273,128]{2,0,1:T(4,128)S(1)}, u32[]{:S(2)}, u32[]{:S(2)}) collective-permute-start(f32[4,273,128]{2,0,1:T(4,128)S(1)} %copy.31), channel_id=1, source_target_pairs={{0,64},{4,68},{8,72},{12,76},{16,80},{20,84},{24,88},{28,92},{32,9... | collective-permute-start | bytes 1677320 | tf_op jit(solution)/shard_map/ppermute | solution.py:14
  233.6 32.3 %collective-permute-start.6 = (f32[4,273,128]{2,0,1:T(4,128)}, f32[4,273,128]{2,0,1:T(4,128)}, u32[]{:S(2)}, u32[]{:S(2)}) collective-permute-start(f32[4,273,128]{2,0,1:T(4,128)} %copy.33), channel_id=1, source_target_pairs={{0,128},{4,132},{8,136},{12,140},{16,144},{20,148},{24,152},{28,15... | collective-permute-start | bytes 1677320 | tf_op jit(solution)/shard_map/ppermute | solution.py:14
  239.4 37.4 %collective-permute-start.17 = (f32[4,273,128]{2,0,1:T(4,128)S(1)}, f32[4,273,128]{2,0,1:T(4,128)S(1)}, u32[]{:S(2)}, u32[]{:S(2)}) collective-permute-start(f32[4,273,128]{2,0,1:T(4,128)S(1)} %copy.42), channel_id=1, source_target_pairs={{4,0},{8,4},{12,8},{16,12},{20,16},{24,20},{28,24},{32,28},{36,32}... | collective-permute-start | bytes 1677320 | tf_op jit(solution)/shard_map/ppermute | solution.py:14
  267.2 51.6 %collective-permute-start.7 = (f32[4,273,128]{2,0,1:T(4,128)S(1)}, f32[4,273,128]{2,0,1:T(4,128)S(1)}, u32[]{:S(2)}, u32[]{:S(2)}) collective-permute-start(f32[4,273,128]{2,0,1:T(4,128)S(1)} %copy.35), channel_id=1, source_target_pairs={{0,256},{4,260},{8,264},{12,268},{16,272},{20,276},{24,280},{28,28... | collective-permute-start | bytes 1677320 | tf_op jit(solution)/shard_map/ppermute | solution.py:14
  277.0 55.6 %collective-permute-start.18 = (f32[4,273,128]{2,0,1:T(4,128)S(1)}, f32[4,273,128]{2,0,1:T(4,128)S(1)}, u32[]{:S(2)}, u32[]{:S(2)}) collective-permute-start(f32[4,273,128]{2,0,1:T(4,128)S(1)} %copy.44), channel_id=1, source_target_pairs={{8,0},{12,4},{16,8},{20,12},{24,16},{28,20},{32,24},{36,28},{40,32... | collective-permute-start | bytes 1677320 | tf_op jit(solution)/shard_map/ppermute | solution.py:14
  319.0 16.6 %collective-permute-start.8 = (f32[4,273,128]{2,0,1:T(4,128)S(1)}, f32[4,273,128]{2,0,1:T(4,128)S(1)}, u32[]{:S(2)}, u32[]{:S(2)}) collective-permute-start(f32[4,273,128]{2,0,1:T(4,128)S(1)} %copy.37), channel_id=1, source_target_pairs={{0,512},{4,516},{8,520},{12,524},{16,528},{20,532},{24,536},{28,54... | collective-permute-start | bytes 1677320 | tf_op jit(solution)/shard_map/ppermute | solution.py:14
  333.6 33.5 %collective-permute-start.19 = (f32[4,273,128]{2,0,1:T(4,128)}, f32[4,273,128]{2,0,1:T(4,128)}, u32[]{:S(2)}, u32[]{:S(2)}) collective-permute-start(f32[4,273,128]{2,0,1:T(4,128)} %copy.46), channel_id=1, source_target_pairs={{16,0},{20,4},{24,8},{28,12},{32,16},{36,20},{40,24},{44,28},{48,3... | collective-permute-start | bytes 1677320 | tf_op jit(solution)/shard_map/ppermute | solution.py:14
  368.5 22.0 %collective-permute-start.20 = (f32[4,273,128]{2,0,1:T(4,128)S(1)}, f32[4,273,128]{2,0,1:T(4,128)S(1)}, u32[]{:S(2)}, u32[]{:S(2)}) collective-permute-start(f32[4,273,128]{2,0,1:T(4,128)S(1)} %copy.48), channel_id=1, source_target_pairs={{32,0},{36,4},{40,8},{44,12},{48,16},{52,20},{56,24},{60,28},{64,3... | collective-permute-start | bytes 1677320 | tf_op jit(solution)/shard_map/ppermute | solution.py:14
  390.7 70.0 %collective-permute-start.21 = (f32[4,273,128]{2,0,1:T(4,128)S(1)}, f32[4,273,128]{2,0,1:T(4,128)S(1)}, u32[]{:S(2)}, u32[]{:S(2)}) collective-permute-start(f32[4,273,128]{2,0,1:T(4,128)S(1)} %copy.50), channel_id=1, source_target_pairs={{64,0},{68,4},{72,8},{76,12},{80,16},{84,20},{88,24},{92,28},{96,3... | collective-permute-start | bytes 1677320 | tf_op jit(solution)/shard_map/ppermute | solution.py:14
  460.9 24.3 %collective-permute-start.22 = (f32[4,273,128]{2,0,1:T(4,128)S(1)}, f32[4,273,128]{2,0,1:T(4,128)S(1)}, u32[]{:S(2)}, u32[]{:S(2)}) collective-permute-start(f32[4,273,128]{2,0,1:T(4,128)S(1)} %copy.52), channel_id=1, source_target_pairs={{128,0},{132,4},{136,8},{140,12},{144,16},{148,20},{152,24},{156,2... | collective-permute-start | bytes 1677320 | tf_op jit(solution)/shard_map/ppermute | solution.py:14
  485.4 117.6 %copy-start.8 = (bf16[4,256,256]{1,2,0:T(8,128)(2,1)S(1)}, bf16[4,256,256]{1,2,0:T(8,128)(2,1)}, u32[]{:S(2)}) copy-start(bf16[4,256,256]{1,2,0:T(8,128)(2,1)} %get-tuple-element.13) | copy-start | bytes 1572868
  485.4 117.6 %copy-start.14 = (f32[256,512]{0,1:T(8,128)S(1)}, f32[256,512]{0,1:T(8,128)}, u32[]{:S(2)}) copy-start(f32[256,512]{0,1:T(8,128)} %copy-done.13) | copy-start | bytes 1572868
  485.5 115.9 %collective-permute-start.23 = (f32[4,273,128]{2,0,1:T(4,128)S(1)}, f32[4,273,128]{2,0,1:T(4,128)S(1)}, u32[]{:S(2)}, u32[]{:S(2)}) collective-permute-start(f32[4,273,128]{2,0,1:T(4,128)S(1)} %copy.54), channel_id=1, source_target_pairs={{256,0},{260,4},{264,8},{268,12},{272,16},{276,20},{280,24},{284,2... | collective-permute-start | bytes 1677320 | tf_op jit(solution)/shard_map/ppermute | solution.py:14
  601.6 29.6 %collective-permute-start.24 = (f32[4,273,128]{2,0,1:T(4,128)S(1)}, f32[4,273,128]{2,0,1:T(4,128)S(1)}, u32[]{:S(2)}, u32[]{:S(2)}) collective-permute-start(f32[4,273,128]{2,0,1:T(4,128)S(1)} %copy.56), channel_id=1, source_target_pairs={{512,0},{516,4},{520,8},{524,12},{528,16},{532,20},{536,24},{540,2... | collective-permute-start | bytes 1677320 | tf_op jit(solution)/shard_map/ppermute | solution.py:14
  (10 other events, 251.9 us)
Sparse Core Ops, SparseCore 0:
  83.9 29.6 all-gather.1
  338.4 88.5 reduce-scatter.1
where the time goes:
time: 642 us; the launch traced here: 641 us
  waiting for transfers between devices  515 us (80%)
  starting transfers between devices  84.2 us (13%)
  between operations  14.8 us (2%)
  matrix products  9.93 us (2%)
  local copies, waits for them, and re-layouts  9.24 us (1%)
  other arithmetic  8.04 us (1%)
    ppermute x25, waiting for transfers between devices, shifted(): return lax.ppermute(x, axis, pairs)  515 us
    ppermute x25, starting transfers between devices, shifted(): return lax.ppermute(x, axis, pairs)  84.2 us
  transfers between devices with their start and end apart: 27, of which 18 were waited for; matrix products, arithmetic and copies ran while one was open for 3% of the time, Pallas kernels for 0%

commit v1 on v0

v1 whole, which is shorter than its diff:
```python
import functools

import jax
import jax.numpy as jnp
from jax import lax
from jax.experimental import pallas as pl
from jax.experimental.pallas import tpu as pltpu
from jax.sharding import PartitionSpec as P

FEAT = 16
VDIM = 128
CONV = 3
NY, NZ, NX = 8, 12, 4
TOK = 256
ROWS = 160
GROUPS = ROWS // 16
NORM = GROUPS
HALO = 16
BF = jnp.bfloat16
F32 = jnp.float32


def mm(a, b):
    return jnp.dot(a, b, preferred_element_type=F32)


def mm_t(a, b):
    return lax.dot_general(a, b, (((1,), (1,)), ((), ())), preferred_element_type=F32)


def remote(src, dst, send, recv, ctx, head):
    return pltpu.make_async_remote_copy(
        src_ref=src,
        dst_ref=dst,
        send_sem=send,
        recv_sem=recv,
        device_id=(ctx, head),
        device_id_type=pl.DeviceIdType.MESH,
    )


def build_features(raw, row0, query, store):
    s = raw[pl.ds(row0, FEAT), :] * FEAT ** (-0.25)
    half = 0.5**0.5
    pair = 2.0 * half if query else half
    store[0:16, :] = s * s * half
    for d in range(1, 8):
        store[16 * d : 16 * d + 16, :] = s * pltpu.roll(s, FEAT - d, 0) * pair
    store[128:136, :] = s[0:8] * s[8:16] * pair
    row = lax.broadcasted_iota(jnp.int32, (8, s.shape[1]), 0)
    store[136:144, :] = jnp.where(row == 0, 1.0, 0.0)
    store[144:160, :] = s


def body(
    q_hbm, k_hbm, v_hbm, ck_ref, cv_ref, w_hbm, cot_hbm, mixed_ref, vgrad_ref,
    qb, kb, vb, w, cotg, raw, feat, q_pt, q_tp, k_pt, k_tp, vc, wl, wlt, dsum,
    state0, total, a1, n1, r1, rn, tsum, tnorm, ry, ryn, base, basen, qo, qn, pr, pn,
    og, ogs, grad, u1, a2, r2, t2, ry2, qo2, pr2, att, atts, vgs,
    rs1s, rs1r, rs2s, rs2r,
    loc, ex_s, ex_r, halo_s, halo_r, p1_s, p1_r, y_s, y_r, p3_s, p3_r,
    g1_s, g1_r, gy_s, gy_r, g3_s, g3_r, ag_s, ag_r, rs_s, rs_r, misc_s, misc_r,
):
    ctx = lax.axis_index("ctx")
    x = lax.axis_index("head")
    y = lax.div(ctx, 2 * NZ)
    chip = lax.div(ctx, 2)
    z = lax.rem(chip, NZ)
    c = lax.rem(ctx, 2)
    sib = chip * 2 + 1 - c
    chips = NY * NZ
    before = lax.rem(chip + chips - 1, chips)
    after = lax.rem(chip + 1, chips)
    right, left = lax.rem(x + 1, NX), lax.rem(x + NX - 1, NX)
    far = lax.rem(x + 2, NX)

    def at(y_, z_):
        return (y_ * NZ + z_) * 2 + c

    load_w = pltpu.make_async_copy(w_hbm, w, loc.at[0])
    load_w.start()
    mine = pl.ds(pl.multiple_of(HALO + TOK * c, 16), TOK)
    own_lanes = pl.ds(pl.multiple_of(256 * c, 256), 256)
    sib_lanes = pl.ds(pl.multiple_of(256 * (1 - c), 256), 256)
    load_k = pltpu.make_async_copy(k_hbm, kb.at[mine, :], loc.at[1])
    load_v = pltpu.make_async_copy(v_hbm.at[:, own_lanes], vb.at[mine, :], loc.at[2])
    load_q = pltpu.make_async_copy(q_hbm, qb.at[c], loc.at[3])
    load_c = pltpu.make_async_copy(cot_hbm, cotg.at[x], loc.at[4])
    for copy in (load_k, load_v, load_q, load_c):
        copy.start()

    barrier = pltpu.get_barrier_semaphore()

    def greet(ctx_, x_):
        pl.semaphore_signal(
            barrier, inc=1, device_id=(ctx_, x_), device_id_type=pl.DeviceIdType.MESH
        )

    greet(sib, x)
    greet(before * 2 + 1, x)
    greet(ctx, right)
    greet(ctx, left)
    for d in range(1, NZ):
        greet(at(y, lax.rem(z + d, NZ)), x)
    for d in range(1, NY):
        greet(at(lax.rem(y + d, NY), z), x)
    pl.semaphore_wait(barrier, 3 + (NZ - 1) + (NY - 1) + 2 * c)

    ex = [
        remote(k_hbm, kb.at[mine, :], ex_s.at[0], ex_r.at[0], sib, x),
        remote(v_hbm.at[:, sib_lanes], vb.at[mine, :], ex_s.at[1], ex_r.at[1], sib, x),
        remote(q_hbm, qb.at[c], ex_s.at[2], ex_r.at[2], sib, x),
    ]
    last = pl.ds(TOK - HALO, HALO)
    halos = []
    for cc in range(2):
        halos.append(
            remote(k_hbm.at[last, :], kb.at[0:HALO, :], halo_s.at[cc], halo_r.at[0], after * 2 + cc, x)
        )
        halos.append(
            remote(
                v_hbm.at[last, 256 * cc : 256 * cc + 256], vb.at[0:HALO, :],
                halo_s.at[2 + cc], halo_r.at[1], after * 2 + cc, x,
            )
        )

    @pl.when(c == 1)
    def _():
        for copy in halos:
            copy.start()

    for copy in ex:
        copy.start()
    ag_right = remote(cot_hbm, cotg.at[x], ag_s.at[0], ag_r.at[0], ctx, right)
    ag_left = remote(cot_hbm, cotg.at[x], ag_s.at[1], ag_r.at[1], ctx, left)
    ag_right.start()
    ag_left.start()

    load_k.wait()
    load_v.wait()
    load_q.wait()
    for copy in ex:
        copy.wait_recv()
    halos[0].wait_recv()
    halos[1].wait_recv()

    @pl.when(chip == 0)
    def _():
        kb[0:HALO, :] = jnp.zeros((HALO, kb.shape[1]), BF)
        vb[0:HALO, :] = jnp.zeros((HALO, vb.shape[1]), BF)

    def convolve(joined, taps):
        out = taps[0:1] * joined[HALO:]
        for j in range(1, CONV):
            out = out + taps[j : j + 1] * pltpu.roll(joined, j, 0)[HALO:]
        return out

    vc[...] = convolve(vb[...].astype(F32), cv_ref[:, own_lanes]).astype(BF)
    key_conv = convolve(kb[...].astype(F32), ck_ref[...])
    queries = jnp.concatenate([qb[0], qb[1]], 0).astype(F32)
    raw[...] = jnp.concatenate([queries, key_conv], 1).T
    heads_row = pl.multiple_of(32 * c, 32)
    for j in range(2):
        build_features(raw, 64 + heads_row + 16 * j, False, feat)
        k_pt[j] = feat[...].astype(BF)
        k_tp[j] = feat[...].T.astype(BF)
        lanes = slice(VDIM * j, VDIM * j + VDIM)
        s0 = mm(k_pt[j, :, 0:TOK], vc[0:TOK, lanes])
        state0[:, lanes] = s0
        a1[:, lanes] = (s0 + mm(k_pt[j, :, TOK:], vc[TOK:, lanes])).astype(BF)
    pick = lax.broadcasted_iota(jnp.int32, (8, 2 * TOK), 0)
    token = lax.broadcasted_iota(jnp.int32, (8, 2 * TOK), 1)
    norms = jnp.zeros((8, ROWS), F32)
    for j in range(2):
        chosen = (pick == j) | ((pick == 2 + j) & (token < TOK))
        norms = norms + mm(jnp.where(chosen, 1.0, 0.0).astype(BF), k_tp[j])
    n1[...] = jnp.zeros(n1.shape, F32)
    n1[:, 0:ROWS] = norms

    def group(ref, g):
        return ref.at[pl.ds(pl.multiple_of(16 * g, 16), 16), :]

    def spread(source, landing, sends, recvs, with_norm):
        for d in range(1, NZ):
            to = lax.rem(z + d, NZ)

            @pl.when(to < GROUPS)
            def _():
                remote(
                    group(source, to), landing.at[z], sends.at[d], recvs.at[z], at(y, to), x
                ).start()

            if with_norm:

                @pl.when(to == NORM)
                def _():
                    remote(n1, rn.at[z], sends.at[d], recvs.at[z], at(y, to), x).start()

    def spread_end(source, landing, sends, recvs, with_norm):
        for d in range(1, NZ):
            to = lax.rem(z + d, NZ)

            @pl.when(to < GROUPS)
            def _():
                remote(
                    group(source, to), landing.at[z], sends.at[d], recvs.at[z], at(y, to), x
                ).wait_send()

            if with_norm:

                @pl.when(to == NORM)
                def _():
                    remote(n1, rn.at[z], sends.at[d], recvs.at[z], at(y, to), x).wait_send()

    def sum_up(source, landing, recvs, sums, ys, yr, landing_y, forward):
        landing[z] = source
        for d in range(1, NZ):
            frm = lax.rem(z + d, NZ)
            remote(sums, landing.at[frm], ys.at[0], recvs.at[frm], ctx, x).wait_recv()
        acc = landing[0].astype(F32)
        for j in range(1, NZ):
            acc = acc + landing[j].astype(F32)
        sums[...] = acc.astype(sums.dtype)
        for d in range(1, NY):
            to = y + d if forward else y - d
            need = to < NY if forward else to >= 0

            @pl.when(need)
            def _():
                remote(sums, landing_y.at[y], ys.at[d], yr.at[y], at(to, z), x).start()

    def hand_out(landing, sums, ys, yr, landing_y, start, outs, forward, send_one, keep_own):
        start[...] = jnp.zeros(start.shape, F32)
        for d in range(1, NY):
            frm = y - d if forward else y + d
            there = frm >= 0 if forward else frm < NY

            @pl.when(there)
            def _():
                remote(sums, landing_y.at[frm], ys.at[0], yr.at[frm], ctx, x).wait_recv()
                start[...] += landing_y[frm].astype(F32)

        run = start[...]
        order = range(NZ) if forward else range(NZ - 1, -1, -1)
        for j in order:
            outs[j] = run.astype(outs.dtype)
            run = run + landing[j].astype(F32)
        for d in range(1, NZ):
            send_one(d, lax.rem(z + d, NZ)).start()
        keep_own(outs[z])

    def y_end(sums, ys, yr, landing_y, forward):
        for d in range(1, NY):
            to = y + d if forward else y - d
            need = to < NY if forward else to >= 0

            @pl.when(need)
            def _():
                remote(sums, landing_y.at[y], ys.at[d], yr.at[y], at(to, z), x).wait_send()

    spread(a1, r1, p1_s, p1_r, True)

    for j in range(2):
        build_features(raw, heads_row + 16 * j, True, feat)
        q_pt[j] = feat[...].astype(BF)
        q_tp[j] = feat[...].T.astype(BF)
    t_at = lax.broadcasted_iota(jnp.int32, (TOK, TOK), 0)
    s_at = lax.broadcasted_iota(jnp.int32, (TOK, TOK), 1)
    for j in range(2):
        for b in range(2):
            rows = slice(TOK * b, TOK * b + TOK)
            scores = jnp.where(t_at >= s_at, mm(q_tp[j, rows], k_pt[j, :, rows]), 0.0)
            wl[j, b] = scores.astype(BF)
            dsum[j, rows] = jnp.sum(scores, 1, keepdims=True)

    @pl.when(z < GROUPS)
    def _():
        sum_up(group(a1, z)[...], r1, p1_r, tsum, y_s, y_r, ry, True)

    @pl.when(z == NORM)
    def _():
        sum_up(n1[...], rn, p1_r, tnorm, y_s, y_r, ryn, True)

    upper, lower = slice(0, TOK // 2), slice(TOK // 2, TOK)
    ag_right.wait_recv()
    ag2_right = remote(
        cotg.at[left, upper], cotg.at[left, upper], ag_s.at[2], ag_r.at[2], ctx, right
    )
    ag2_right.start()
    ag_left.wait_recv()
    ag2_left = remote(
        cotg.at[right, lower], cotg.at[right, lower], ag_s.at[3], ag_r.at[3], ctx, left
    )
    ag2_left.start()

    for j in range(2):
        for b in range(2):
            rows = slice(TOK * b, TOK * b + TOK)
            flipped = jnp.where(s_at >= t_at, mm(k_tp[j, rows], q_pt[j, :, rows]), 0.0)
            wlt[j, b] = flipped.astype(BF)

    def out_state(d, to):
        return remote(qo.at[to], group(pr, z), p3_s.at[d], p3_r.at[z], at(y, to), x)

    def out_norm(d, to):
        return remote(qn.at[to], pn, p3_s.at[d], p3_r.at[z], at(y, to), x)

    def keep_state(value):
        group(pr, z)[...] = value

    def keep_norm(value):
        pn[...] = value

    @pl.when(z < GROUPS)
    def _():
        hand_out(r1, tsum, y_s, y_r, ry, base, qo, True, out_state, keep_state)

    @pl.when(z == NORM)
    def _():
        hand_out(rn, tnorm, y_s, y_r, ryn, basen, qn, True, out_norm, keep_norm)

    load_w.wait()
    load_c.wait()
    remote(cotg.at[far, upper], cotg.at[far, upper], ag_s.at[2], ag_r.at[2], ctx, right).wait_recv()
    remote(cotg.at[far, lower], cotg.at[far, lower], ag_s.at[3], ag_r.at[3], ctx, left).wait_recv()

    def out_grad(row0):
        acc = None
        for i in range(NX):
            part = mm_t(cotg[i], w[pl.ds(row0, 256), 512 * i : 512 * i + 512])
            acc = part if acc is None else acc + part
        return acc

    ogs[...] = out_grad(pl.multiple_of(256 * (1 - c), 256))
    og_copy = remote(ogs, og.at[c], misc_s.at[0], misc_r.at[0], sib, x)
    og_copy.start()
    og[c] = out_grad(pl.multiple_of(256 * c, 256))

    for j in range(GROUPS):

        @pl.when(z != j)
        def _():
            remote(qo.at[0], pr.at[16 * j : 16 * j + 16, :], p3_s.at[0], p3_r.at[j], ctx, x).wait_recv()

    @pl.when(z != NORM)
    def _():
        remote(qn.at[0], pn, p3_s.at[0], p3_r.at[NORM], ctx, x).wait_recv()

    og_copy.wait_recv()
    for b in range(2):
        rows = slice(TOK * b, TOK * b + TOK)
        for j in range(2):
            lanes = slice(VDIM * j, VDIM * j + VDIM)
            norm = pn[j : j + 1, 0:ROWS]
            if b == 1:
                norm = norm + n1[2 + j : 3 + j, 0:ROWS]
            there = jnp.sum(q_tp[j, rows].astype(F32) * norm, 1, keepdims=True)
            inverse = 1.0 / (dsum[j, rows] + there)
            dsum[j, rows] = inverse
            grad[rows, lanes] = (og[b, :, lanes] * inverse).astype(BF)
    for j in range(2):
        lanes = slice(VDIM * j, VDIM * j + VDIM)
        later = mm(q_pt[j, :, TOK:], grad[TOK:, lanes])
        u1[:, lanes] = later
        a2[:, lanes] = (later + mm(q_pt[j, :, 0:TOK], grad[0:TOK, lanes])).astype(BF)
    spread(a2, r2, g1_s, g1_r, False)

    total[...] = (pr[...].astype(F32) + state0[...]).astype(BF)
    for b in range(2):
        rows = slice(TOK * b, TOK * b + TOK)
        prior = pr if b == 0 else total
        parts = []
        for j in range(2):
            lanes = slice(VDIM * j, VDIM * j + VDIM)
            numerator = mm(wl[j, b], vc[rows, lanes]) + mm(q_tp[j, rows], prior[:, lanes])
            parts.append((numerator * dsum[j, rows]).astype(BF))
        atts[b] = jnp.concatenate(parts, 1)
    at_copy = remote(atts.at[1 - c], att.at[c], misc_s.at[1], misc_r.at[1], sib, x)
    at_copy.start()
    att[c] = atts[c]

    @pl.when(z < GROUPS)
    def _():
        sum_up(group(a2, z)[...], r2, g1_r, t2, gy_s, gy_r, ry2, False)

    at_copy.wait_recv()

    def project(to):
        columns = pl.ds(pl.multiple_of(512 * to, 512), 512)
        return mm(att[0], w[0:256, columns]) + mm(att[1], w[256:512, columns])

    part = project(far)
    rs1s[0] = part[upper].astype(BF)
    rs1s[1] = part[lower].astype(BF)
    rs1 = [
        remote(rs1s.at[0], rs1r.at[0], rs_s.at[0], rs_r.at[0], ctx, right),
        remote(rs1s.at[1], rs1r.at[1], rs_s.at[1], rs_r.at[1], ctx, left),
    ]
    rs1[0].start()
    rs1[1].start()

    def out_later(d, to):
        return remote(qo2.at[to], group(pr2, z), g3_s.at[d], g3_r.at[z], at(y, to), x)

    def keep_later(value):
        group(pr2, z)[...] = value

    @pl.when(z < GROUPS)
    def _():
        hand_out(r2, t2, gy_s, gy_r, ry2, base, qo2, False, out_later, keep_later)

    to_right = project(right)
    to_left = project(left)
    rs1[0].wait_recv()
    rs2s[0, upper] = (to_right[upper] + rs1r[0].astype(F32)).astype(BF)
    rs2s[0, lower] = to_right[lower].astype(BF)
    rs2_right = remote(rs2s.at[0], rs2r.at[0], rs_s.at[2], rs_r.at[2], ctx, right)
    rs2_right.start()
    rs1[1].wait_recv()
    rs2s[1, lower] = (to_left[lower] + rs1r[1].astype(F32)).astype(BF)
    rs2s[1, upper] = to_left[upper].astype(BF)
    rs2_left = remote(rs2s.at[1], rs2r.at[1], rs_s.at[3], rs_r.at[3], ctx, left)
    rs2_left.start()
    here = project(x)

    for j in range(GROUPS):

        @pl.when(z != j)
        def _():
            remote(qo2.at[0], pr2.at[16 * j : 16 * j + 16, :], g3_s.at[0], g3_r.at[j], ctx, x).wait_recv()

    total[...] = (pr2[...].astype(F32) + u1[...]).astype(BF)
    for b in range(2):
        rows = slice(TOK * b, TOK * b + TOK)
        later = total if b == 0 else pr2
        parts = []
        for j in range(2):
            lanes = slice(VDIM * j, VDIM * j + VDIM)
            value = mm(wlt[j, b], grad[rows, lanes]) + mm(k_tp[j, rows], later[:, lanes])
            parts.append(value.astype(BF))
        vgs[b] = jnp.concatenate(parts, 1)
    vg_copy = remote(vgs.at[1 - c], vgrad_ref.at[:, own_lanes], misc_s.at[2], misc_r.at[2], sib, x)
    vg_copy.start()
    vgrad_ref[:, own_lanes] = vgs[c]

    rs2_right.wait_recv()
    rs2_left.wait_recv()
    mixed_ref[...] = (here + rs2r[0].astype(F32) + rs2r[1].astype(F32)).astype(BF)

    for copy in ex:
        copy.wait_send()

    @pl.when(c == 1)
    def _():
        for copy in halos:
            copy.wait_send()

    for copy in (ag_right, ag_left, ag2_right, ag2_left, og_copy, at_copy, rs1[0], rs1[1], rs2_right, rs2_left):
        copy.wait_send()
    spread_end(a1, r1, p1_s, p1_r, True)
    spread_end(a2, r2, g1_s, g1_r, False)

    @pl.when(z < GROUPS)
    def _():
        y_end(tsum, y_s, y_r, ry, True)
        y_end(t2, gy_s, gy_r, ry2, False)
        for d in range(1, NZ):
            out_state(d, lax.rem(z + d, NZ)).wait_send()
            out_later(d, lax.rem(z + d, NZ)).wait_send()

    @pl.when(z == NORM)
    def _():
        y_end(tnorm, y_s, y_r, ryn, True)
        for d in range(1, NZ):
            out_norm(d, lax.rem(z + d, NZ)).wait_send()

    vg_copy.wait_send()
    vg_copy.wait_recv()


def per_device(queries, keys, values, conv_keys, conv_values, out_weight, cotangent):
    vmem = pltpu.VMEM
    dma = pltpu.SemaphoreType.DMA
    both = 2 * TOK
    scratch = [
        vmem((2, TOK, 64), BF),
        vmem((HALO + both, 64), BF),
        vmem((HALO + both, 256), BF),
        vmem((512, 2048), BF),
        vmem((NX, TOK, 512), BF),
        vmem((128, both), F32),
        vmem((ROWS, both), F32),
        vmem((2, ROWS, both), BF),
        vmem((2, both, ROWS), BF),
        vmem((2, ROWS, both), BF),
        vmem((2, both, ROWS), BF),
        vmem((both, 256), BF),
        vmem((2, 2, TOK, TOK), BF),
        vmem((2, 2, TOK, TOK), BF),
        vmem((2, both, 1), F32),
        vmem((ROWS, 256), F32),
        vmem((ROWS, 256), BF),
        vmem((ROWS, 256), BF),
        vmem((8, 256), F32),
        vmem((NZ, 16, 256), BF),
        vmem((NZ, 8, 256), F32),
        vmem((16, 256), BF),
        vmem((8, 256), F32),
        vmem((NY, 16, 256), BF),
        vmem((NY, 8, 256), F32),
        vmem((16, 256), F32),
        vmem((8, 256), F32),
        vmem((NZ, 16, 256), BF),
        vmem((NZ, 8, 256), F32),
        vmem((ROWS, 256), BF),
        vmem((8, 256), F32),
        vmem((2, TOK, 256), F32),
        vmem((TOK, 256), F32),
        vmem((both, 256), BF),
        vmem((ROWS, 256), F32),
        vmem((ROWS, 256), BF),
        vmem((NZ, 16, 256), BF),
        vmem((16, 256), BF),
        vmem((NY, 16, 256), BF),
        vmem((NZ, 16, 256), BF),
        vmem((ROWS, 256), BF),
        vmem((2, TOK, 256), BF),
        vmem((2, TOK, 256), BF),
        vmem((2, TOK, 256), BF),
        vmem((2, TOK // 2, 512), BF),
        vmem((2, TOK // 2, 512), BF),
        vmem((2, TOK, 512), BF),
        vmem((2, TOK, 512), BF),
        dma((5,)),
        dma((3,)), dma((3,)),
        dma((4,)), dma((2,)),
        dma((NZ,)), dma((NZ,)), dma((NY,)), dma((NY,)), dma((NZ,)), dma((NZ,)),
        dma((NZ,)), dma((NZ,)), dma((NY,)), dma((NY,)), dma((NZ,)), dma((NZ,)),
        dma((4,)), dma((4,)), dma((4,)), dma((4,)), dma((3,)), dma((3,)),
    ]
    in_hbm = pl.BlockSpec(memory_space=pl.ANY)
    in_vmem = pl.BlockSpec(memory_space=pltpu.VMEM)
    out = jax.ShapeDtypeStruct(values.shape, BF)
    return pl.pallas_call(
        body,
        out_shape=(out, out),
        in_specs=[in_hbm, in_hbm, in_hbm, in_vmem, in_vmem, in_hbm, in_hbm],
        out_specs=(in_vmem, in_vmem),
        scratch_shapes=scratch,
        compiler_params=pltpu.CompilerParams(
            collective_id=0, has_side_effects=True, vmem_limit_bytes=48 << 20
        ),
    )(queries, keys, values, conv_keys, conv_values, out_weight, cotangent)


def solution(mesh):
    in_specs = (
        P("ctx", "head"),
        P("ctx", "head"),
        P("ctx", "head"),
        P(None, "head"),
        P(None, "head"),
        P("head", None),
        P("ctx", "head"),
    )
    out_specs = (P("ctx", "head"), P("ctx", "head"))
    return jax.shard_map(
        per_device, mesh=mesh, in_specs=in_specs, out_specs=out_specs, check_vma=False
    )
```

time: 642 us -> 74.2 us (0.12)
  the two profiles are of different devices: /device:TPU:22 before, /device:TPU:1 now
where the time goes in v1:
time: 74.2 us; the launch traced here: 73.6 us
  Pallas kernels  64.9 us (87%)
  local copies, waits for them, and re-layouts  8.02 us (11%)
    pallas_call x1, Pallas kernels, per_device(): pl.pallas_call(body, out_shape=(out, out), in_specs=[in_hbm, in_hbm, in_h...  64.9 us
    unnamed x14, local copies, waits for them, and re-layouts  8.02 us

profile of v1, /device:TPU:1, one launch (start us, length us, event | category | flops | bytes accessed | tf_op | source)
XLA Modules:
  0.0 73.6 jit_solution(6481603586442847618)
XLA Ops:
  0.6 0.9 %copy.9.q_hbm = bf16[256,64]{1,0:T(8,128)(2,1)S(1)} copy(bf16[256,64]{0,1:T(8,128)(2,1)} %param.7) | data formatting | bytes 65536 | tf_op args[0]
  1.5 0.9 %copy.10.k_hbm = bf16[256,64]{1,0:T(8,128)(2,1)S(1)} copy(bf16[256,64]{0,1:T(8,128)(2,1)} %param.8) | data formatting | bytes 65536 | tf_op args[1]
  2.4 0.0 copy-start
  2.4 1.6 %copy-done = bf16[512,2048]{1,0:T(8,128)(2,1)S(1)} copy-done((bf16[512,2048]{1,0:T(8,128)(2,1)S(1)}, bf16[512,2048]{1,0:T(8,128)(2,1)}, u32[]{:S(2)}) %copy-start) | copy-done | bytes 2097176
  4.0 0.0 copy-start.1
  4.0 0.9 %copy-done.1 = bf16[256,512]{1,0:T(8,128)(2,1)S(1)} copy-done((bf16[256,512]{1,0:T(8,128)(2,1)S(1)}, bf16[256,512]{1,0:T(8,128)(2,1)}, u32[]{:S(2)}) %copy-start.1) | copy-done | bytes 262168
  4.9 0.0 copy-start.2
  4.9 0.9 %copy-done.2 = bf16[256,512]{1,0:T(8,128)(2,1)S(1)} copy-done((bf16[256,512]{1,0:T(8,128)(2,1)S(1)}, bf16[256,512]{1,0:T(8,128)(2,1)}, u32[]{:S(2)}) %copy-start.2) | copy-done | bytes 262168
  5.9 0.0 copy-start.3
  5.9 0.7 copy-done.3
  6.6 0.0 copy-start.4
  6.6 0.7 copy-done.4
  7.3 64.9 %shard_map.86 = (bf16[256,512]{1,0:T(8,128)(2,1)S(1)}, bf16[256,512]{1,0:T(8,128)(2,1)S(1)}) custom-call(bf16[256,64]{1,0:T(8,128)(2,1)S(1)} %copy.9.q_hbm, bf16[256,64]{1,0:T(8,128)(2,1)S(1)} %copy.10.k_hbm, bf16[256,512]{1,0:T(8,128)(2,1)S(1)} %copy-done.1, f32[3,64]{1,0:T(4,128)S(1)} %copy-done.4, f32[3,512]{1,0:T(4,128)S(1)} %copy-done.3, ...), custom_call_target="tpu_custom_call" | custom-call | tf_op jit(solution)/shard_map/pallas_call | solution.py:544
  72.2 0.7 copy.13
  72.9 0.7 copy.14
Async XLA Ops:
  2.4 1.6 %copy-start = (bf16[512,2048]{1,0:T(8,128)(2,1)S(1)}, bf16[512,2048]{1,0:T(8,128)(2,1)}, u32[]{:S(2)}) copy-start(bf16[512,2048]{1,0:T(8,128)(2,1)} %w_hbm.1) | copy-start | bytes 6291460
  4.0 0.9 %copy-start.1 = (bf16[256,512]{1,0:T(8,128)(2,1)S(1)}, bf16[256,512]{1,0:T(8,128)(2,1)}, u32[]{:S(2)}) copy-start(bf16[256,512]{1,0:T(8,128)(2,1)} %v_hbm.1) | copy-start | bytes 786436
  4.9 0.9 %copy-start.2 = (bf16[256,512]{1,0:T(8,128)(2,1)S(1)}, bf16[256,512]{1,0:T(8,128)(2,1)}, u32[]{:S(2)}) copy-start(bf16[256,512]{1,0:T(8,128)(2,1)} %cot_hbm.1) | copy-start | bytes 786436
  5.9 0.7 copy-start.3
  6.6 0.7 copy-start.4

commit v2 on v1

v2 whole, which is shorter than its diff:
```python
import functools

import jax
import jax.numpy as jnp
from jax import lax
from jax.experimental import pallas as pl
from jax.experimental.pallas import tpu as pltpu
from jax.sharding import PartitionSpec as P

FEAT = 16
VDIM = 128
CONV = 3
NY, NZ, NX = 8, 12, 4
TOK = 256
ROWS = 160
GROUPS = ROWS // 16
HALO = 16
ALONG_Z = sorted(range(1, NZ), key=lambda d: -min(d, NZ - d))
ALONG_Y = sorted(range(1, NY), key=lambda d: -min(d, NY - d))
BF = jnp.bfloat16
F32 = jnp.float32


def mm(a, b):
    return jnp.dot(a, b, preferred_element_type=F32)


def mm_t(a, b):
    return lax.dot_general(a, b, (((1,), (1,)), ((), ())), preferred_element_type=F32)


def remote(src, dst, send, recv, ctx, head):
    return pltpu.make_async_remote_copy(
        src_ref=src,
        dst_ref=dst,
        send_sem=send,
        recv_sem=recv,
        device_id=(ctx, head),
        device_id_type=pl.DeviceIdType.MESH,
    )


def build_features(channels, query, store):
    s = channels * FEAT ** (-0.25)
    half = 0.5**0.5
    pair = 2.0 * half if query else half
    store[0:16, :] = s * s * half
    for d in range(1, 8):
        store[16 * d : 16 * d + 16, :] = s * pltpu.roll(s, FEAT - d, 0) * pair
    store[128:136, :] = s[0:8] * s[8:16] * pair
    row = lax.broadcasted_iota(jnp.int32, (8, s.shape[1]), 0)
    store[136:144, :] = jnp.where(row == 0, 1.0, 0.0)
    store[144:160, :] = s


def body(
    q_hbm, k_hbm, v_hbm, ck_hbm, cv_hbm, w_hbm, cot_hbm, mixed_ref, vgrad_ref,
    ck, cv, taps, qb, kb, vb, w, cotg, feat, q_pt, q_tp, k_pt, k_tp, vc, wl, dsum,
    state0, total, a1, n1, own0, nz, nt, ny, r1, tsum, ry, base, qo, pr,
    og, ogs, grad, vin, u1, a2, r2, t2, ry2, qo2, pr2, atts, vgs,
    attg, wcol,
    loc, ex_s, ex_r, halo_s, halo_r, p1_s, p1_r, y_s, y_r, p3_s, p3_r,
    g1_s, g1_r, gy_s, gy_r, g3_s, g3_r, ag_s, ag_r, nz_s, nz_r, ny_s, ny_r, wc_s, wc_r, wf_s, wf_r, at_s, at_r, misc_s, misc_r,
):
    ctx = lax.axis_index("ctx")
    x = lax.axis_index("head")
    y = lax.div(ctx, 2 * NZ)
    chip = lax.div(ctx, 2)
    z = lax.rem(chip, NZ)
    c = lax.rem(ctx, 2)
    sib = chip * 2 + 1 - c
    chips = NY * NZ
    before = lax.rem(chip + chips - 1, chips)
    after = lax.rem(chip + 1, chips)
    right, left = lax.rem(x + 1, NX), lax.rem(x + NX - 1, NX)
    far = lax.rem(x + 2, NX)

    def at(y_, z_):
        return (y_ * NZ + z_) * 2 + c

    sent, due = [], {}

    def go(copy, name=None):
        copy.start()
        sent.append(copy.wait_send)
        if name is not None:
            due[name] = copy.wait_recv
        return copy

    def arrived(name):
        due.pop(name)()

    def finish():
        for name in list(due):
            arrived(name)
        for wait in sent:
            wait()

    own_lanes = pl.ds(pl.multiple_of(256 * c, 256), 256)
    sib_lanes = pl.ds(pl.multiple_of(256 * (1 - c), 256), 256)
    own_rows = pl.ds(pl.multiple_of(32 * c, 32), 32)
    sib_rows = pl.ds(pl.multiple_of(32 * (1 - c), 32), 32)
    mine = pl.ds(pl.multiple_of(HALO + TOK * c, 16), TOK)
    mine_k = pl.ds(pl.multiple_of(128 + TOK * c, 128), TOK)
    loads = [
        pltpu.make_async_copy(ck_hbm, ck, loc.at[5]),
        pltpu.make_async_copy(cv_hbm.at[:, own_lanes], cv, loc.at[6]),
        pltpu.make_async_copy(k_hbm.at[own_rows, :], kb.at[:, mine_k], loc.at[1]),
        pltpu.make_async_copy(q_hbm.at[own_rows, :], qb.at[:, own_lanes], loc.at[3]),
        pltpu.make_async_copy(v_hbm.at[:, own_lanes], vb.at[mine, :], loc.at[2]),
    ]
    for copy in loads:
        copy.start()
    load_c = pltpu.make_async_copy(cot_hbm, cotg.at[x], loc.at[4])
    load_w = pltpu.make_async_copy(w_hbm, w, loc.at[0])
    load_c.start()
    load_w.start()
    due["c"] = load_c.wait
    due["w"] = load_w.wait

    barrier = pltpu.get_barrier_semaphore()

    def greet(ctx_, x_):
        pl.semaphore_signal(
            barrier, inc=1, device_id=(ctx_, x_), device_id_type=pl.DeviceIdType.MESH
        )

    for d in ALONG_Z:
        greet(at(y, lax.rem(z + d, NZ)), x)
    for d in ALONG_Y:
        greet(at(lax.rem(y + d, NY), z), x)
    greet(ctx, far)
    greet(before * 2 + 1, x)
    greet(ctx, right)
    greet(ctx, left)
    greet(sib, x)
    pl.semaphore_wait(barrier, 4 + (NZ - 1) + (NY - 1) + 2 * c)

    last = pl.ds(TOK - HALO, HALO)
    halos = []
    for cc in range(2):
        halos.append(
            remote(
                k_hbm.at[32 * cc : 32 * cc + 32, TOK - 128 : TOK], kb.at[:, 0:128],
                halo_s.at[cc], halo_r.at[0], after * 2 + cc, x,
            )
        )
        halos.append(
            remote(
                v_hbm.at[last, 256 * cc : 256 * cc + 256], vb.at[0:HALO, :],
                halo_s.at[2 + cc], halo_r.at[1], after * 2 + cc, x,
            )
        )

    @pl.when(c == 1)
    def _():
        for copy in halos:
            copy.start()

    def halos_left():
        @pl.when(c == 1)
        def _():
            for copy in halos:
                copy.wait_send()

    sent.append(halos_left)
    due["halo_k"] = halos[0].wait_recv
    due["halo_v"] = halos[1].wait_recv
    go(remote(k_hbm.at[sib_rows, :], kb.at[:, mine_k], ex_s.at[0], ex_r.at[0], sib, x), "k")
    go(remote(v_hbm.at[:, sib_lanes], vb.at[mine, :], ex_s.at[1], ex_r.at[1], sib, x), "v")
    go(remote(q_hbm.at[sib_rows, :], qb.at[:, own_lanes], ex_s.at[2], ex_r.at[2], sib, x), "q")
    def gather(own, slots, sends, recvs, name):
        go(remote(own(0), slots(x, 0), sends.at[0], recvs.at[0], ctx, right), name + "_left0")
        go(remote(own(1), slots(x, 1), sends.at[1], recvs.at[1], ctx, left), name + "_right1")
        go(remote(own(1), slots(x, 1), sends.at[2], recvs.at[2], ctx, right), name + "_left1")
        go(remote(own(0), slots(x, 0), sends.at[3], recvs.at[3], ctx, left), name + "_right0")

    def pass_on(slots, sends, recvs, name):
        arrived(name + "_left0")
        go(remote(slots(left, 0), slots(left, 0), sends.at[4], recvs.at[4], ctx, right), name + "_far0")
        arrived(name + "_right1")
        go(remote(slots(right, 1), slots(right, 1), sends.at[5], recvs.at[5], ctx, left), name + "_far1")

    cot_half = lambda i: pl.ds(TOK // 2 * i, TOK // 2)
    cot_slot = lambda who, i: cotg.at[who, cot_half(i)]
    gather(lambda i: cot_hbm.at[cot_half(i), :], cot_slot, ag_s, ag_r, "cot")

    for copy in loads:
        copy.wait()
    for name in ("k", "halo_k", "v", "halo_v"):
        arrived(name)

    @pl.when(chip == 0)
    def _():
        kb[:, 0:128] = jnp.zeros((32, 128), BF)
        vb[0:HALO, :] = jnp.zeros((HALO, 256), BF)

    taps[...] = jnp.zeros(taps.shape, F32)
    taps[0:CONV, 0:64] = ck[...]
    taps[...] = taps[...].T
    tap = taps[own_rows, :]
    joined = kb[...].astype(F32)
    key_conv = tap[:, 0:1] * joined[:, 128:]
    for j in range(1, CONV):
        key_conv = key_conv + tap[:, j : j + 1] * pltpu.roll(joined, j, 1)[:, 128:]
    for j in range(2):
        build_features(key_conv[16 * j : 16 * j + 16], False, feat)
        k_pt[j] = feat[...].astype(BF)
        k_tp[j] = feat[...].T.astype(BF)
    pick = lax.broadcasted_iota(jnp.int32, (8, 2 * TOK), 0)
    token = lax.broadcasted_iota(jnp.int32, (8, 2 * TOK), 1)
    ones = jnp.where((pick == 0) | ((pick == 1) & (token < TOK)), 1.0, 0.0).astype(BF)
    n1[...] = jnp.zeros(n1.shape, F32)
    for j in range(2):
        norms = mm(ones, k_tp[j])
        n1[2 * j : 2 * j + 1, :] = norms[0:1, 0:128]
        n1[2 * j + 1 : 2 * j + 2, 0 : ROWS - 128] = norms[0:1, 128:]
        own0[j] = norms
    for d in ALONG_Z:
        to = lax.rem(z + d, NZ)
        go(remote(n1, nz.at[z], nz_s.at[d], nz_r.at[z], at(y, to), x))
    nz[z] = n1[...]

    joined = vb[...].astype(F32)
    value_conv = cv[0:1] * joined[HALO:]
    for j in range(1, CONV):
        value_conv = value_conv + cv[j : j + 1] * pltpu.roll(joined, j, 0)[HALO:]
    vc[...] = value_conv.astype(BF)
    for j in range(2):
        lanes = slice(VDIM * j, VDIM * j + VDIM)
        s0 = mm(k_pt[j, :, 0:TOK], vc[0:TOK, lanes])
        state0[:, lanes] = s0
        a1[:, lanes] = (s0 + mm(k_pt[j, :, TOK:], vc[TOK:, lanes])).astype(BF)

    def group(ref, g):
        return ref.at[pl.ds(pl.multiple_of(16 * g, 16), 16), :]

    def spread(source, landing, sends, recvs):
        for d in ALONG_Z:
            to = lax.rem(z + d, NZ)

            @pl.when(to < GROUPS)
            def _():
                remote(
                    group(source, to), landing.at[z], sends.at[d], recvs.at[z], at(y, to), x
                ).start()

    def spread_end(source, landing, sends, recvs):
        for d in ALONG_Z:
            to = lax.rem(z + d, NZ)

            @pl.when(to < GROUPS)
            def _():
                remote(
                    group(source, to), landing.at[z], sends.at[d], recvs.at[z], at(y, to), x
                ).wait_send()

    def sum_up(source, source_like, landing, recvs, sums, ys, yr, landing_y, forward):
        landing[z] = source
        for d in ALONG_Z:
            frm = lax.rem(z + d, NZ)
            remote(source_like, landing.at[frm], ys.at[0], recvs.at[frm], ctx, x).wait_recv()
        acc = landing[0].astype(F32)
        for j in range(1, NZ):
            acc = acc + landing[j].astype(F32)
        sums[...] = acc.astype(sums.dtype)
        for d in ALONG_Y:
            to = y + d if forward else y - d
            need = to < NY if forward else to >= 0

            @pl.when(need)
            def _():
                remote(sums, landing_y.at[y], ys.at[d], yr.at[y], at(to, z), x).start()

    def hand_out(landing, sums, ys, yr, landing_y, start, outs, forward, send_one, keep_own):
        start[...] = jnp.zeros(start.shape, F32)
        for d in ALONG_Y:
            frm = y - d if forward else y + d
            there = frm >= 0 if forward else frm < NY

            @pl.when(there)
            def _():
                remote(sums, landing_y.at[frm], ys.at[0], yr.at[frm], ctx, x).wait_recv()
                start[...] += landing_y[frm].astype(F32)

        run = start[...]
        order = range(NZ) if forward else range(NZ - 1, -1, -1)
        for j in order:
            outs[j] = run.astype(outs.dtype)
            run = run + landing[j].astype(F32)
        for d in ALONG_Z:
            send_one(d, lax.rem(z + d, NZ)).start()
        keep_own(outs[z])

    def y_end(sums, ys, yr, landing_y, forward):
        for d in ALONG_Y:
            to = y + d if forward else y - d
            need = to < NY if forward else to >= 0

            @pl.when(need)
            def _():
                remote(sums, landing_y.at[y], ys.at[d], yr.at[y], at(to, z), x).wait_send()

    spread(a1, r1, p1_s, p1_r)
    sent.append(lambda: spread_end(a1, r1, p1_s, p1_r))

    arrived("q")
    for j in range(2):
        build_features(qb[16 * j : 16 * j + 16, :].astype(F32), True, feat)
        q_pt[j] = feat[...].astype(BF)
        q_tp[j] = feat[...].T.astype(BF)
    t_at = lax.broadcasted_iota(jnp.int32, (TOK, TOK), 0)
    s_at = lax.broadcasted_iota(jnp.int32, (TOK, TOK), 1)
    for j in range(2):
        for b in range(2):
            rows = slice(TOK * b, TOK * b + TOK)
            scores = jnp.where(t_at >= s_at, mm(q_tp[j, rows], k_pt[j, :, rows]), 0.0)
            wl[j, b] = scores.astype(BF)
            dsum[j, rows] = jnp.sum(scores, 1, keepdims=True)

    pass_on(cot_slot, ag_s, ag_r, "cot")

    for d in ALONG_Z:
        frm = lax.rem(z + d, NZ)
        remote(n1, nz.at[frm], nz_s.at[0], nz_r.at[frm], ctx, x).wait_recv()
    acc = nz[0]
    for j in range(1, NZ):
        acc = acc + nz[j]
    nt[...] = acc
    for d in ALONG_Y:

        @pl.when(y + d < NY)
        def _():
            remote(nt, ny.at[y], ny_s.at[d], ny_r.at[y], at(y + d, z), x).start()

    def norms_left():
        for d in ALONG_Y:

            @pl.when(y + d < NY)
            def _():
                remote(nt, ny.at[y], ny_s.at[d], ny_r.at[y], at(y + d, z), x).wait_send()

    sent.append(norms_left)

    half = pl.ds(pl.multiple_of(256 * c, 256), 256)
    for d in (1, 3, 2):
        to = lax.rem(x + d, NX)
        columns = pl.ds(pl.multiple_of(512 * to, 512), 512)
        go(remote(w_hbm.at[half, columns], wcol.at[x, half], wc_s.at[d], wc_r.at[d], ctx, to))
    load_wc = pltpu.make_async_copy(
        w_hbm.at[:, pl.ds(pl.multiple_of(512 * x, 512), 512)], wcol.at[x], loc.at[7]
    )
    load_wc.start()

    arrived("c")
    arrived("w")

    def out_grad(who, row0):
        columns = pl.ds(pl.multiple_of(512 * who, 512), 512)
        return mm_t(cotg[who], w[pl.ds(row0, 256), columns])

    own_row = pl.multiple_of(256 * c, 256)
    sib_row = pl.multiple_of(256 * (1 - c), 256)
    for name in ("cot_left1", "cot_right0"):
        arrived(name)
    ogs[...] = out_grad(x, sib_row) + out_grad(left, sib_row) + out_grad(right, sib_row)
    og[c] = out_grad(x, own_row) + out_grad(left, own_row) + out_grad(right, own_row)

    @pl.when(z < GROUPS)
    def _():
        sum_up(group(a1, z)[...], group(a1, z), r1, p1_r, tsum, y_s, y_r, ry, True)

    arrived("cot_far0")
    arrived("cot_far1")
    ogs[...] += out_grad(far, sib_row)
    go(remote(ogs, og.at[c], misc_s.at[0], misc_r.at[0], sib, x), "og")
    og[c] += out_grad(far, own_row)

    base_n = jnp.zeros((4, 128), F32)
    for j in range(NZ):
        base_n = base_n + jnp.where(j < z, nz[j], 0.0)
    for j in range(NY):

        @pl.when(j >= y)
        def _():
            ny[j] = jnp.zeros((4, 128), F32)

        @pl.when(j < y)
        def _():
            remote(nt, ny.at[j], ny_s.at[0], ny_r.at[j], ctx, x).wait_recv()

    for j in range(NY):
        base_n = base_n + ny[j]
    arrived("og")
    for b in range(2):
        rows = slice(TOK * b, TOK * b + TOK)
        for j in range(2):
            lanes = slice(VDIM * j, VDIM * j + VDIM)
            norm = jnp.concatenate(
                [base_n[2 * j : 2 * j + 1], base_n[2 * j + 1 : 2 * j + 2, 0 : ROWS - 128]], 1
            )
            if b == 1:
                norm = norm + own0[j, 1:2]
            there = jnp.sum(q_tp[j, rows].astype(F32) * norm, 1, keepdims=True)
            inverse = 1.0 / (dsum[j, rows] + there)
            dsum[j, rows] = inverse
            grad[rows, lanes] = (og[b, :, lanes] * inverse).astype(BF)
    for j in range(2):
        lanes = slice(VDIM * j, VDIM * j + VDIM)
        later = mm(q_pt[j, :, TOK:], grad[TOK:, lanes])
        u1[:, lanes] = later
        a2[:, lanes] = (later + mm(q_pt[j, :, 0:TOK], grad[0:TOK, lanes])).astype(BF)
    spread(a2, r2, g1_s, g1_r)
    sent.append(lambda: spread_end(a2, r2, g1_s, g1_r))

    def out_state(d, to):
        return remote(qo.at[to], group(pr, z), p3_s.at[d], p3_r.at[z], at(y, to), x)

    def keep_state(value):
        group(pr, z)[...] = value

    @pl.when(z < GROUPS)
    def _():
        hand_out(r1, tsum, y_s, y_r, ry, base, qo, True, out_state, keep_state)

    for d in (1, 3, 2):
        frm = lax.rem(x + NX - d, NX)
        remote(
            w_hbm.at[half, 0:512], wcol.at[frm, half], wc_s.at[d], wc_r.at[d], ctx, x
        ).wait_recv()
        go(
            remote(wcol.at[frm, half], wcol.at[frm, half], wf_s.at[d], wf_r.at[d], sib, x),
            "wcol%d" % d,
        )

    for j in range(2):
        lanes = slice(VDIM * j, VDIM * j + VDIM)
        for b in range(2):
            rows = slice(TOK * b, TOK * b + TOK)
            flipped = jnp.where(s_at >= t_at, mm(k_tp[j, rows], q_pt[j, :, rows]), 0.0)
            vin[rows, lanes] = mm(flipped.astype(BF), grad[rows, lanes])

    @pl.when(z < GROUPS)
    def _():
        sum_up(group(a2, z)[...], group(a2, z), r2, g1_r, t2, gy_s, gy_r, ry2, False)

    for j in range(GROUPS):

        @pl.when(z != j)
        def _():
            remote(
                qo.at[0], pr.at[16 * j : 16 * j + 16, :], p3_s.at[0], p3_r.at[j], ctx, x
            ).wait_recv()

    total[...] = (pr[...].astype(F32) + state0[...]).astype(BF)
    for b in range(2):
        rows = slice(TOK * b, TOK * b + TOK)
        prior = pr if b == 0 else total
        parts = []
        for j in range(2):
            lanes = slice(VDIM * j, VDIM * j + VDIM)
            numerator = mm(wl[j, b], vc[rows, lanes]) + mm(q_tp[j, rows], prior[:, lanes])
            parts.append((numerator * dsum[j, rows]).astype(BF))
        atts[b] = jnp.concatenate(parts, 1)
    go(remote(atts.at[1 - c], attg.at[x, c], misc_s.at[1], misc_r.at[1], sib, x), "att")
    attg[x, c] = atts[c]
    arrived("att")
    att_slot = lambda who, i: attg.at[who, i]
    gather(lambda i: attg.at[x, i], att_slot, at_s, at_r, "att")

    def out_later(d, to):
        return remote(qo2.at[to], group(pr2, z), g3_s.at[d], g3_r.at[z], at(y, to), x)

    def keep_later(value):
        group(pr2, z)[...] = value

    @pl.when(z < GROUPS)
    def _():
        hand_out(r2, t2, gy_s, gy_r, ry2, base, qo2, False, out_later, keep_later)

    load_wc.wait()
    for d in (1, 3, 2):
        arrived("wcol%d" % d)

    def project(frm):
        return mm(attg[frm, 0], wcol[frm, 0:256]) + mm(attg[frm, 1], wcol[frm, 256:512])

    mixed = project(x)
    pass_on(att_slot, at_s, at_r, "att")

    for j in range(GROUPS):

        @pl.when(z != j)
        def _():
            remote(
                qo2.at[0], pr2.at[16 * j : 16 * j + 16, :], g3_s.at[0], g3_r.at[j], ctx, x
            ).wait_recv()

    total[...] = (pr2[...].astype(F32) + u1[...]).astype(BF)
    for b in range(2):
        rows = slice(TOK * b, TOK * b + TOK)
        later = total if b == 0 else pr2
        parts = []
        for j in range(2):
            lanes = slice(VDIM * j, VDIM * j + VDIM)
            value = vin[rows, lanes] + mm(k_tp[j, rows], later[:, lanes])
            parts.append(value.astype(BF))
        vgs[b] = jnp.concatenate(parts, 1)
    go(
        remote(vgs.at[1 - c], vgrad_ref.at[:, own_lanes], misc_s.at[2], misc_r.at[2], sib, x),
        "value_grad",
    )
    vgrad_ref[:, own_lanes] = vgs[c]

    for who, name in ((left, "left"), (right, "right"), (far, "far")):
        arrived("att_" + name + "1") if name != "right" else arrived("att_right0")
        if name == "far":
            arrived("att_far0")
        mixed = mixed + project(who)
    mixed_ref[...] = mixed.astype(BF)

    def scans_left():
        @pl.when(z < GROUPS)
        def _():
            y_end(tsum, y_s, y_r, ry, True)
            y_end(t2, gy_s, gy_r, ry2, False)
            for d in ALONG_Z:
                out_state(d, lax.rem(z + d, NZ)).wait_send()
                out_later(d, lax.rem(z + d, NZ)).wait_send()

    sent.append(scans_left)
    finish()


def per_device(queries, keys, values, conv_keys, conv_values, out_weight, cotangent):
    vmem = pltpu.VMEM
    dma = pltpu.SemaphoreType.DMA
    both = 2 * TOK
    scratch = [
        vmem((CONV, 64), F32),
        vmem((CONV, 256), F32),
        vmem((128, 128), F32),
        vmem((32, both), BF),
        vmem((32, 128 + both), BF),
        vmem((HALO + both, 256), BF),
        vmem((512, 2048), BF),
        vmem((NX, TOK, 512), BF),
        vmem((ROWS, both), F32),
        vmem((2, ROWS, both), BF),
        vmem((2, both, ROWS), BF),
        vmem((2, ROWS, both), BF),
        vmem((2, both, ROWS), BF),
        vmem((both, 256), BF),
        vmem((2, 2, TOK, TOK), BF),
        vmem((2, both, 1), F32),
        vmem((ROWS, 256), F32),
        vmem((ROWS, 256), BF),
        vmem((ROWS, 256), BF),
        vmem((4, 128), F32),
        vmem((2, 8, ROWS), F32),
        vmem((NZ, 4, 128), F32),
        vmem((4, 128), F32),
        vmem((NY, 4, 128), F32),
        vmem((NZ, 16, 256), BF),
        vmem((16, 256), F32),
        vmem((NY, 16, 256), F32),
        vmem((16, 256), F32),
        vmem((NZ, 16, 256), BF),
        vmem((ROWS, 256), BF),
        vmem((2, TOK, 256), F32),
        vmem((TOK, 256), F32),
        vmem((both, 256), BF),
        vmem((both, 256), F32),
        vmem((ROWS, 256), F32),
        vmem((ROWS, 256), BF),
        vmem((NZ, 16, 256), BF),
        vmem((16, 256), BF),
        vmem((NY, 16, 256), BF),
        vmem((NZ, 16, 256), BF),
        vmem((ROWS, 256), BF),
        vmem((2, TOK, 256), BF),
        vmem((2, TOK, 256), BF),
        vmem((NX, 2, TOK, 256), BF),
        vmem((NX, 512, 512), BF),
        dma((8,)),
        dma((3,)), dma((3,)),
        dma((4,)), dma((2,)),
        dma((NZ,)), dma((NZ,)), dma((NY,)), dma((NY,)), dma((NZ,)), dma((NZ,)),
        dma((NZ,)), dma((NZ,)), dma((NY,)), dma((NY,)), dma((NZ,)), dma((NZ,)),
        dma((6,)), dma((6,)),
        dma((NZ,)), dma((NZ,)), dma((NY,)), dma((NY,)),
        dma((NX,)), dma((NX,)), dma((NX,)), dma((NX,)), dma((6,)), dma((6,)),
        dma((3,)), dma((3,)),
    ]
    in_hbm = pl.BlockSpec(memory_space=pltpu.HBM)
    in_vmem = pl.BlockSpec(memory_space=pltpu.VMEM)
    out = jax.ShapeDtypeStruct(values.shape, BF)
    return pl.pallas_call(
        body,
        out_shape=(out, out),
        in_specs=[in_hbm] * 7,
        out_specs=(in_vmem, in_vmem),
        scratch_shapes=scratch,
        compiler_params=pltpu.CompilerParams(
            collective_id=0, has_side_effects=True, vmem_limit_bytes=56 << 20
        ),
    )(queries.T, keys.T, values, conv_keys, conv_values, out_weight, cotangent)


def solution(mesh):
    in_specs = (
        P("ctx", "head"),
        P("ctx", "head"),
        P("ctx", "head"),
        P(None, "head"),
        P(None, "head"),
        P("head", None),
        P("ctx", "head"),
    )
    out_specs = (P("ctx", "head"), P("ctx", "head"))
    return jax.shard_map(
        per_device, mesh=mesh, in_specs=in_specs, out_specs=out_specs, check_vma=False
    )
```

time: 74.2 us -> 62.8 us (0.85)
  Pallas kernels: 64.9 us -> 58.6 us
  local copies, waits for them, and re-layouts: 8.02 us -> 3.34 us
    pallas_call x1, Pallas kernels: 64.9 us -> 58.6 us  [per_device(): pl.pallas_call(body, out_shape=(out, out), in_specs=[in_hbm] * 7, out_spe...]
    unnamed x14 -> x2, local copies, waits for them, and re-layouts: 8.02 us -> 3.34 us
where the time goes in v2:
time: 62.8 us; the launch traced here: 62.6 us
  Pallas kernels  58.6 us (93%)
  local copies, waits for them, and re-layouts  3.34 us (5%)
  between operations  0.64 us (1%)
    pallas_call x1, Pallas kernels, per_device(): pl.pallas_call(body, out_shape=(out, out), in_specs=[in_hbm] * 7, out_spe...  58.6 us
    unnamed x2, local copies, waits for them, and re-layouts  3.34 us

profile of v2, /device:TPU:1, one launch (start us, length us, event | category | flops | bytes accessed | tf_op | source)
XLA Modules:
  0.0 62.6 jit_solution(14071862798313707278)
XLA Ops:
  0.6 58.6 %shard_map.86 = (bf16[256,512]{1,0:T(8,128)(2,1)}, bf16[256,512]{1,0:T(8,128)(2,1)}) custom-call(bf16[64,256]{1,0:T(8,128)(2,1)} %bitcast.2, bf16[64,256]{1,0:T(8,128)(2,1)} %bitcast.3, bf16[256,512]{1,0:T(8,128)(2,1)} %v_hbm.1, f32[3,64]{1,0:T(4,128)} %ck_hbm.1, f32[3,512]{1,0:T(4,128)} %cv_hbm.1, bf16[512,2048]{1,0:T(8,128)(2,1)} %w_hbm.1, ...), custom_call_target="tpu_custom_call" | custom-call | tf_op jit(solution)/shard_map/pallas_call | solution.py:598
  59.3 1.7 %copy.11 = bf16[256,512]{1,0:T(8,128)(2,1)} copy(bf16[256,512]{1,0:T(8,128)(2,1)} %get-tuple-element.4) | data formatting | bytes 524288
  61.0 1.7 %copy.12 = bf16[256,512]{1,0:T(8,128)(2,1)} copy(bf16[256,512]{1,0:T(8,128)(2,1)} %get-tuple-element.5) | data formatting | bytes 524288

commit v3 on v2

--- a/solution.py
+++ b/solution.py
@@ -54,10 +54,10 @@
 
 
 def body(
-    q_hbm, k_hbm, v_hbm, ck_hbm, cv_hbm, w_hbm, cot_hbm, mixed_ref, vgrad_ref,
+    q_hbm, k_hbm, v_hbm, ck_hbm, cv_hbm, w_hbm, cot_hbm, out_ref,
     ck, cv, taps, qb, kb, vb, w, cotg, feat, q_pt, q_tp, k_pt, k_tp, vc, wl, dsum,
-    state0, total, a1, n1, own0, nz, nt, ny, r1, tsum, ry, base, qo, pr,
-    og, ogs, grad, vin, u1, a2, r2, t2, ry2, qo2, pr2, atts, vgs,
+    state0, a1, n1, own0, nz, nt, ny, r1, tsum, ry, base, qo, pr,
+    og, ogs, grad, vin, u1, a2, r2, t2, ry2, qo2, pr2, atts, pri, numi, vgs, lat,
     attg, wcol,
     loc, ex_s, ex_r, halo_s, halo_r, p1_s, p1_r, y_s, y_r, p3_s, p3_r,
     g1_s, g1_r, gy_s, gy_r, g3_s, g3_r, ag_s, ag_r, nz_s, nz_r, ny_s, ny_r, wc_s, wc_r, wf_s, wf_r, at_s, at_r, misc_s, misc_r,
@@ -78,6 +78,22 @@
     def at(y_, z_):
         return (y_ * NZ + z_) * 2 + c
 
+    barrier = pltpu.get_barrier_semaphore()
+
+    def greet(ctx_, x_):
+        pl.semaphore_signal(
+            barrier, inc=1, device_id=(ctx_, x_), device_id_type=pl.DeviceIdType.MESH
+        )
+
+    for d in ALONG_Z:
+        greet(at(y, lax.rem(z + d, NZ)), x)
+    for d in ALONG_Y:
+        greet(at(lax.rem(y + d, NY), z), x)
+    greet(ctx, far)
+    greet(before * 2 + 1, x)
+    greet(ctx, right)
+    greet(ctx, left)
+    greet(sib, x)
     sent, due = [], {}
 
     def go(copy, name=None):
@@ -98,6 +114,7 @@
 
     own_lanes = pl.ds(pl.multiple_of(256 * c, 256), 256)
     sib_lanes = pl.ds(pl.multiple_of(256 * (1 - c), 256), 256)
+    vg_lanes = pl.ds(pl.multiple_of(512 + 256 * c, 256), 256)
     own_rows = pl.ds(pl.multiple_of(32 * c, 32), 32)
     sib_rows = pl.ds(pl.multiple_of(32 * (1 - c), 32), 32)
     mine = pl.ds(pl.multiple_of(HALO + TOK * c, 16), TOK)
@@ -118,22 +135,6 @@
     due["c"] = load_c.wait
     due["w"] = load_w.wait
 
-    barrier = pltpu.get_barrier_semaphore()
-
-    def greet(ctx_, x_):
-        pl.semaphore_signal(
-            barrier, inc=1, device_id=(ctx_, x_), device_id_type=pl.DeviceIdType.MESH
-        )
-
-    for d in ALONG_Z:
-        greet(at(y, lax.rem(z + d, NZ)), x)
-    for d in ALONG_Y:
-        greet(at(lax.rem(y + d, NY), z), x)
-    greet(ctx, far)
-    greet(before * 2 + 1, x)
-    greet(ctx, right)
-    greet(ctx, left)
-    greet(sib, x)
     pl.semaphore_wait(barrier, 4 + (NZ - 1) + (NY - 1) + 2 * c)
 
     last = pl.ds(TOK - HALO, HALO)
@@ -187,32 +188,41 @@
 
     for copy in loads:
         copy.wait()
-    for name in ("k", "halo_k", "v", "halo_v"):
+    for name in ("k", "v"):
         arrived(name)
+
+    taps[...] = jnp.zeros(taps.shape, F32)
+    taps[0:CONV, 0:64] = ck[...]
+    taps[...] = taps[...].T
+    tap = taps[own_rows, :]
+
+    def key_features(joined, columns):
+        key_conv = tap[:, 0:1] * joined[:, 128:]
+        for j in range(1, CONV):
+            key_conv = key_conv + tap[:, j : j + 1] * pltpu.roll(joined, j, 1)[:, 128:]
+        for j in range(2):
+            build_features(key_conv[16 * j : 16 * j + 16], False, feat.at[j, :, columns])
+            k_pt[j, :, columns] = feat[j, :, columns].astype(BF)
+
+    key_features(
+        jnp.concatenate([jnp.zeros((32, 128), F32), kb[:, 128:].astype(F32)], 1),
+        slice(0, 2 * TOK),
+    )
+    arrived("halo_k")
+    arrived("halo_v")
 
     @pl.when(chip == 0)
     def _():
         kb[:, 0:128] = jnp.zeros((32, 128), BF)
         vb[0:HALO, :] = jnp.zeros((HALO, 256), BF)
 
-    taps[...] = jnp.zeros(taps.shape, F32)
-    taps[0:CONV, 0:64] = ck[...]
-    taps[...] = taps[...].T
-    tap = taps[own_rows, :]
-    joined = kb[...].astype(F32)
-    key_conv = tap[:, 0:1] * joined[:, 128:]
-    for j in range(1, CONV):
-        key_conv = key_conv + tap[:, j : j + 1] * pltpu.roll(joined, j, 1)[:, 128:]
-    for j in range(2):
-        build_features(key_conv[16 * j : 16 * j + 16], False, feat)
-        k_pt[j] = feat[...].astype(BF)
-        k_tp[j] = feat[...].T.astype(BF)
+    key_features(kb[:, 0:256].astype(F32), slice(0, 128))
     pick = lax.broadcasted_iota(jnp.int32, (8, 2 * TOK), 0)
     token = lax.broadcasted_iota(jnp.int32, (8, 2 * TOK), 1)
     ones = jnp.where((pick == 0) | ((pick == 1) & (token < TOK)), 1.0, 0.0).astype(BF)
     n1[...] = jnp.zeros(n1.shape, F32)
     for j in range(2):
-        norms = mm(ones, k_tp[j])
+        norms = mm_t(ones, k_pt[j])
         n1[2 * j : 2 * j + 1, :] = norms[0:1, 0:128]
         n1[2 * j + 1 : 2 * j + 2, 0 : ROWS - 128] = norms[0:1, 128:]
         own0[j] = norms
@@ -304,11 +314,13 @@
     spread(a1, r1, p1_s, p1_r)
     sent.append(lambda: spread_end(a1, r1, p1_s, p1_r))
 
+    for j in range(2):
+        k_tp[j] = feat[j].T.astype(BF)
     arrived("q")
     for j in range(2):
-        build_features(qb[16 * j : 16 * j + 16, :].astype(F32), True, feat)
-        q_pt[j] = feat[...].astype(BF)
-        q_tp[j] = feat[...].T.astype(BF)
+        build_features(qb[16 * j : 16 * j + 16, :].astype(F32), True, feat.at[j])
+        q_pt[j] = feat[j].astype(BF)
+        q_tp[j] = feat[j].T.astype(BF)
     t_at = lax.broadcasted_iota(jnp.int32, (TOK, TOK), 0)
     s_at = lax.broadcasted_iota(jnp.int32, (TOK, TOK), 1)
     for j in range(2):
@@ -423,6 +435,60 @@
     def _():
         hand_out(r1, tsum, y_s, y_r, ry, base, qo, True, out_state, keep_state)
 
+    for j in range(2):
+        lanes = slice(VDIM * j, VDIM * j + VDIM)
+        for b in range(2):
+            rows = slice(TOK * b, TOK * b + TOK)
+            flipped = jnp.where(s_at >= t_at, mm(k_tp[j, rows], q_pt[j, :, rows]), 0.0)
+            vin[rows, lanes] = mm(flipped.astype(BF), grad[rows, lanes])
+
+    for j in range(2):
+        lanes = slice(VDIM * j, VDIM * j + VDIM)
+        for b in range(2):
+            rows = slice(TOK * b, TOK * b + TOK)
+            numi[rows, lanes] = mm(wl[j, b], vc[rows, lanes])
+
+    @pl.when(z < GROUPS)
+    def _():
+        sum_up(group(a2, z)[...], group(a2, z), r2, g1_r, t2, gy_s, gy_r, ry2, False)
+
+    for j in range(GROUPS):
+
+        @pl.when(z != j)
+        def _():
+            remote(
+                qo.at[0], pr.at[16 * j : 16 * j + 16, :], p3_s.at[0], p3_r.at[j], ctx, x
+            ).wait_recv()
+
+    pri[0] = pr[...]
+    pri[1] = (pr[...].astype(F32) + state0[...]).astype(BF)
+
+    def attend(b):
+        rows = pl.ds(pl.multiple_of(TOK * b, TOK), TOK)
+        parts = []
+        for j in range(2):
+            lanes = slice(VDIM * j, VDIM * j + VDIM)
+            numerator = numi[rows, lanes] + mm(q_tp[j, rows], pri[b, :, lanes])
+            parts.append((numerator * dsum[j, rows]).astype(BF))
+        return jnp.concatenate(parts, 1)
+
+    atts[...] = attend(1 - c)
+    go(remote(atts, attg.at[x, c], misc_s.at[1], misc_r.at[1], sib, x), "att")
+    attg[x, c] = attend(c)
+    arrived("att")
+    att_slot = lambda who, i: attg.at[who, i]
+    gather(lambda i: attg.at[x, i], att_slot, at_s, at_r, "att")
+
+    def out_later(d, to):
+        return remote(qo2.at[to], group(pr2, z), g3_s.at[d], g3_r.at[z], at(y, to), x)
+
+    def keep_later(value):
+        group(pr2, z)[...] = value
+
+    @pl.when(z < GROUPS)
+    def _():
+        hand_out(r2, t2, gy_s, gy_r, ry2, base, qo2, False, out_later, keep_later)
+
     for d in (1, 3, 2):
         frm = lax.rem(x + NX - d, NX)
         remote(
@@ -433,51 +499,6 @@
             "wcol%d" % d,
         )
 
-    for j in range(2):
-        lanes = slice(VDIM * j, VDIM * j + VDIM)
-        for b in range(2):
-            rows = slice(TOK * b, TOK * b + TOK)
-            flipped = jnp.where(s_at >= t_at, mm(k_tp[j, rows], q_pt[j, :, rows]), 0.0)
-            vin[rows, lanes] = mm(flipped.astype(BF), grad[rows, lanes])
-
-    @pl.when(z < GROUPS)
-    def _():
-        sum_up(group(a2, z)[...], group(a2, z), r2, g1_r, t2, gy_s, gy_r, ry2, False)
-
-    for j in range(GROUPS):
-
-        @pl.when(z != j)
-        def _():
-            remote(
-                qo.at[0], pr.at[16 * j : 16 * j + 16, :], p3_s.at[0], p3_r.at[j], ctx, x
-            ).wait_recv()
-
-    total[...] = (pr[...].astype(F32) + state0[...]).astype(BF)
-    for b in range(2):
-        rows = slice(TOK * b, TOK * b + TOK)
-        prior = pr if b == 0 else total
-        parts = []
-        for j in range(2):
-            lanes = slice(VDIM * j, VDIM * j + VDIM)
-            numerator = mm(wl[j, b], vc[rows, lanes]) + mm(q_tp[j, rows], prior[:, lanes])
-            parts.append((numerator * dsum[j, rows]).astype(BF))
-        atts[b] = jnp.concatenate(parts, 1)
-    go(remote(atts.at[1 - c], attg.at[x, c], misc_s.at[1], misc_r.at[1], sib, x), "att")
-    attg[x, c] = atts[c]
-    arrived("att")
-    att_slot = lambda who, i: attg.at[who, i]
-    gather(lambda i: attg.at[x, i], att_slot, at_s, at_r, "att")
-
-    def out_later(d, to):
-        return remote(qo2.at[to], group(pr2, z), g3_s.at[d], g3_r.at[z], at(y, to), x)
-
-    def keep_later(value):
-        group(pr2, z)[...] = value
-
-    @pl.when(z < GROUPS)
-    def _():
-        hand_out(r2, t2, gy_s, gy_r, ry2, base, qo2, False, out_later, keep_later)
-
     load_wc.wait()
     for d in (1, 3, 2):
         arrived("wcol%d" % d)
@@ -496,28 +517,32 @@
                 qo2.at[0], pr2.at[16 * j : 16 * j + 16, :], g3_s.at[0], g3_r.at[j], ctx, x
             ).wait_recv()
 
-    total[...] = (pr2[...].astype(F32) + u1[...]).astype(BF)
-    for b in range(2):
-        rows = slice(TOK * b, TOK * b + TOK)
-        later = total if b == 0 else pr2
+    lat[0] = (pr2[...].astype(F32) + u1[...]).astype(BF)
+    lat[1] = pr2[...]
+
+    def value_grad(b):
+        rows = pl.ds(pl.multiple_of(TOK * b, TOK), TOK)
         parts = []
         for j in range(2):
             lanes = slice(VDIM * j, VDIM * j + VDIM)
-            value = vin[rows, lanes] + mm(k_tp[j, rows], later[:, lanes])
+            value = vin[rows, lanes] + mm(k_tp[j, rows], lat[b, :, lanes])
             parts.append(value.astype(BF))
-        vgs[b] = jnp.concatenate(parts, 1)
+        return jnp.concatenate(parts, 1)
+
+    vgs[...] = value_grad(1 - c)
     go(
-        remote(vgs.at[1 - c], vgrad_ref.at[:, own_lanes], misc_s.at[2], misc_r.at[2], sib, x),
+        remote(vgs, out_ref.at[:, vg_lanes], misc_s.at[2], misc_r.at[2], sib, x),
         "value_grad",
     )
-    vgrad_ref[:, own_lanes] = vgs[c]
-
-    for who, name in ((left, "left"), (right, "right"), (far, "far")):
-        arrived("att_" + name + "1") if name != "right" else arrived("att_right0")
-        if name == "far":
-            arrived("att_far0")
+    out_ref[:, vg_lanes] = value_grad(c)
+
+    for who, name in ((left, "att_left1"), (right, "att_right0")):
+        arrived(name)
         mixed = mixed + project(who)
-    mixed_ref[...] = mixed.astype(BF)
+    for name in ("att_far0", "att_far1"):
+        arrived(name)
+    mixed = mixed + project(far)
+    out_ref[:, 0:512] = mixed.astype(BF)
 
     def scans_left():
         @pl.when(z < GROUPS)
@@ -545,7 +570,7 @@
         vmem((HALO + both, 256), BF),
         vmem((512, 2048), BF),
         vmem((NX, TOK, 512), BF),
-        vmem((ROWS, both), F32),
+        vmem((2, ROWS, both), F32),
         vmem((2, ROWS, both), BF),
         vmem((2, both, ROWS), BF),
         vmem((2, ROWS, both), BF),
@@ -555,15 +580,14 @@
         vmem((2, both, 1), F32),
         vmem((ROWS, 256), F32),
         vmem((ROWS, 256), BF),
-        vmem((ROWS, 256), BF),
         vmem((4, 128), F32),
         vmem((2, 8, ROWS), F32),
         vmem((NZ, 4, 128), F32),
         vmem((4, 128), F32),
         vmem((NY, 4, 128), F32),
         vmem((NZ, 16, 256), BF),
-        vmem((16, 256), F32),
-        vmem((NY, 16, 256), F32),
+        vmem((16, 256), BF),
+        vmem((NY, 16, 256), BF),
         vmem((16, 256), F32),
         vmem((NZ, 16, 256), BF),
         vmem((ROWS, 256), BF),
@@ -578,8 +602,11 @@
         vmem((NY, 16, 256), BF),
         vmem((NZ, 16, 256), BF),
         vmem((ROWS, 256), BF),
-        vmem((2, TOK, 256), BF),
-        vmem((2, TOK, 256), BF),
+        vmem((TOK, 256), BF),
+        vmem((2, ROWS, 256), BF),
+        vmem((both, 256), F32),
+        vmem((TOK, 256), BF),
+        vmem((2, ROWS, 256), BF),
         vmem((NX, 2, TOK, 256), BF),
         vmem((NX, 512, 512), BF),
         dma((8,)),
@@ -594,17 +621,18 @@
     ]
     in_hbm = pl.BlockSpec(memory_space=pltpu.HBM)
     in_vmem = pl.BlockSpec(memory_space=pltpu.VMEM)
-    out = jax.ShapeDtypeStruct(values.shape, BF)
-    return pl.pallas_call(
+    out = jax.ShapeDtypeStruct((TOK, 1024), BF)
+    both_out = pl.pallas_call(
         body,
-        out_shape=(out, out),
+        out_shape=out,
         in_specs=[in_hbm] * 7,
-        out_specs=(in_vmem, in_vmem),
+        out_specs=in_vmem,
         scratch_shapes=scratch,
         compiler_params=pltpu.CompilerParams(
             collective_id=0, has_side_effects=True, vmem_limit_bytes=56 << 20
         ),
     )(queries.T, keys.T, values, conv_keys, conv_values, out_weight, cotangent)
+    return both_out[:, 0:512], both_out[:, 512:1024]
 
 
 def solution(mesh):

time: 62.8 us -> 59 us (0.939)
  Pallas kernels: 58.6 us -> 56.4 us
  local copies, waits for them, and re-layouts: 3.34 us -> 1.85 us
    unnamed x2 -> x0, local copies, waits for them, and re-layouts: 3.34 us -> none
    pallas_call x1, Pallas kernels: 58.6 us -> 56.4 us  [per_device(): pl.pallas_call(body, out_shape=out, in_specs=[in_hbm] * 7, out_specs=in_v...]
    slice x0 -> x1, local copies, waits for them, and re-layouts: none -> 1.85 us  [per_device(): return (both_out[:, 0:512], both_out[:, 512:1024])]
where the time goes in v3:
time: 59 us; the launch traced here: 58.9 us
  Pallas kernels  56.4 us (96%)
  local copies, waits for them, and re-layouts  1.85 us (3%)
  between operations  0.64 us (1%)
    pallas_call x1, Pallas kernels, per_device(): pl.pallas_call(body, out_shape=out, in_specs=[in_hbm] * 7, out_specs=in_v...  56.4 us
    slice x1, local copies, waits for them, and re-layouts, per_device(): return (both_out[:, 0:512], both_out[:, 512:1024])  1.85 us

profile of v3, /device:TPU:1, one launch (start us, length us, event | category | flops | bytes accessed | tf_op | source)
XLA Modules:
  0.0 58.9 jit_solution(7043813324268997451)
XLA Ops:
  0.6 56.4 %shard_map.86 = bf16[256,1024]{1,0:T(8,128)(2,1)} custom-call(bf16[64,256]{1,0:T(8,128)(2,1)} %bitcast.2, bf16[64,256]{1,0:T(8,128)(2,1)} %bitcast.3, bf16[256,512]{1,0:T(8,128)(2,1)} %v_hbm.1, f32[3,64]{1,0:T(4,128)} %ck_hbm.1, f32[3,512]{1,0:T(4,128)} %cv_hbm.1, bf16[512,2048]{1,0:T(8,128)(2,1)} %w_hbm.1, bf16[256,512]{1,0:T(8,128)(2,1)} %cot_hbm.1), custom_call_target="tpu_custom_call" | custom-call | tf_op jit(solution)/shard_map/pallas_call | solution.py:625
  57.0 1.9 %fusion = (bf16[256,512]{1,0:T(8,128)(2,1)}, bf16[256,512]{1,0:T(8,128)(2,1)}) fusion(bf16[256,1024]{1,0:T(8,128)(2,1)} %shard_map.86), kind=kLoop, calls=%fused_computation | loop fusion | bytes 1048576 | tf_op jit(solution)/shard_map/slice | solution.py:635

commit v4 on v3

--- a/solution.py
+++ b/solution.py
@@ -208,6 +208,16 @@
         jnp.concatenate([jnp.zeros((32, 128), F32), kb[:, 128:].astype(F32)], 1),
         slice(0, 2 * TOK),
     )
+
+    def value_conv(joined):
+        out = cv[0:1] * joined[HALO:]
+        for j in range(1, CONV):
+            out = out + cv[j : j + 1] * pltpu.roll(joined, j, 0)[HALO:]
+        return out.astype(BF)
+
+    vc[...] = value_conv(
+        jnp.concatenate([jnp.zeros((HALO, 256), F32), vb[HALO:, :].astype(F32)], 0)
+    )
     arrived("halo_k")
     arrived("halo_v")
 
@@ -231,11 +241,7 @@
         go(remote(n1, nz.at[z], nz_s.at[d], nz_r.at[z], at(y, to), x))
     nz[z] = n1[...]
 
-    joined = vb[...].astype(F32)
-    value_conv = cv[0:1] * joined[HALO:]
-    for j in range(1, CONV):
-        value_conv = value_conv + cv[j : j + 1] * pltpu.roll(joined, j, 0)[HALO:]
-    vc[...] = value_conv.astype(BF)
+    vc[0:HALO, :] = value_conv(vb[0 : 2 * HALO, :].astype(F32))
     for j in range(2):
         lanes = slice(VDIM * j, VDIM * j + VDIM)
         s0 = mm(k_pt[j, :, 0:TOK], vc[0:TOK, lanes])
@@ -439,13 +445,6 @@
         lanes = slice(VDIM * j, VDIM * j + VDIM)
         for b in range(2):
             rows = slice(TOK * b, TOK * b + TOK)
-            flipped = jnp.where(s_at >= t_at, mm(k_tp[j, rows], q_pt[j, :, rows]), 0.0)
-            vin[rows, lanes] = mm(flipped.astype(BF), grad[rows, lanes])
-
-    for j in range(2):
-        lanes = slice(VDIM * j, VDIM * j + VDIM)
-        for b in range(2):
-            rows = slice(TOK * b, TOK * b + TOK)
             numi[rows, lanes] = mm(wl[j, b], vc[rows, lanes])
 
     @pl.when(z < GROUPS)
@@ -472,12 +471,26 @@
             parts.append((numerator * dsum[j, rows]).astype(BF))
         return jnp.concatenate(parts, 1)
 
+    att_slot = lambda who, i: attg.at[who, i]
+
+    def send_half(i):
+        mine_half = attg.at[x, i]
+        go(remote(mine_half, mine_half, at_s.at[2 * i], at_r.at[2 * i], ctx, right))
+        go(remote(mine_half, mine_half, at_s.at[3 - 2 * i], at_r.at[3 - 2 * i], ctx, left))
+
+    for i in range(2):
+        due["att_left%d" % i] = remote(
+            attg.at[left, i], attg.at[left, i], at_s.at[2 * i], at_r.at[2 * i], ctx, right
+        ).wait_recv
+        due["att_right%d" % i] = remote(
+            attg.at[right, i], attg.at[right, i], at_s.at[3 - 2 * i], at_r.at[3 - 2 * i], ctx, left
+        ).wait_recv
+    attg[x, c] = attend(c)
+    send_half(c)
     atts[...] = attend(1 - c)
     go(remote(atts, attg.at[x, c], misc_s.at[1], misc_r.at[1], sib, x), "att")
-    attg[x, c] = attend(c)
     arrived("att")
-    att_slot = lambda who, i: attg.at[who, i]
-    gather(lambda i: attg.at[x, i], att_slot, at_s, at_r, "att")
+    send_half(1 - c)
 
     def out_later(d, to):
         return remote(qo2.at[to], group(pr2, z), g3_s.at[d], g3_r.at[z], at(y, to), x)
@@ -488,6 +501,14 @@
     @pl.when(z < GROUPS)
     def _():
         hand_out(r2, t2, gy_s, gy_r, ry2, base, qo2, False, out_later, keep_later)
+
+    pass_on(att_slot, at_s, at_r, "att")
+    for j in range(2):
+        lanes = slice(VDIM * j, VDIM * j + VDIM)
+        for b in range(2):
+            rows = slice(TOK * b, TOK * b + TOK)
+            flipped = jnp.where(s_at >= t_at, mm(k_tp[j, rows], q_pt[j, :, rows]), 0.0)
+            vin[rows, lanes] = mm(flipped.astype(BF), grad[rows, lanes])
 
     for d in (1, 3, 2):
         frm = lax.rem(x + NX - d, NX)
@@ -507,7 +528,6 @@
         return mm(attg[frm, 0], wcol[frm, 0:256]) + mm(attg[frm, 1], wcol[frm, 256:512])
 
     mixed = project(x)
-    pass_on(att_slot, at_s, at_r, "att")
 
     for j in range(GROUPS):
 

time: 59 us -> 58.8 us (level)
  no operation moved by 1% of the time
where the time goes in v4:
time: 58.8 us; the launch traced here: 58.6 us
  Pallas kernels  56.1 us (95%)
  local copies, waits for them, and re-layouts  1.85 us (3%)
  between operations  0.64 us (1%)
    pallas_call x1, Pallas kernels, per_device(): pl.pallas_call(body, out_shape=out, in_specs=[in_hbm] * 7, out_specs=in_v...  56.1 us
    slice x1, local copies, waits for them, and re-layouts, per_device(): return (both_out[:, 0:512], both_out[:, 512:1024])  1.85 us

profile of v4, /device:TPU:1, one launch (start us, length us, event | category | flops | bytes accessed | tf_op | source)
XLA Modules:
  0.0 58.6 jit_solution(14813260011524388344)
XLA Ops:
  0.6 56.1 %shard_map.86 = bf16[256,1024]{1,0:T(8,128)(2,1)} custom-call(bf16[64,256]{1,0:T(8,128)(2,1)} %bitcast.2, bf16[64,256]{1,0:T(8,128)(2,1)} %bitcast.3, bf16[256,512]{1,0:T(8,128)(2,1)} %v_hbm.1, f32[3,64]{1,0:T(4,128)} %ck_hbm.1, f32[3,512]{1,0:T(4,128)} %cv_hbm.1, bf16[512,2048]{1,0:T(8,128)(2,1)} %w_hbm.1, bf16[256,512]{1,0:T(8,128)(2,1)} %cot_hbm.1), custom_call_target="tpu_custom_call" | custom-call | tf_op jit(solution)/shard_map/pallas_call | solution.py:645
  56.8 1.9 %fusion = (bf16[256,512]{1,0:T(8,128)(2,1)}, bf16[256,512]{1,0:T(8,128)(2,1)}) fusion(bf16[256,1024]{1,0:T(8,128)(2,1)} %shard_map.86), kind=kLoop, calls=%fused_computation | loop fusion | bytes 1048576 | tf_op jit(solution)/shard_map/slice | solution.py:655
